TPU v7x, 128 devices: a whole 4x4x4 slice. The times are simulated.
128 devices in a mesh: gx: 4 (over z_lo, core), gy: 4 (over y), gz: 8 (over z_hi, x).
Axes of the slice: x: 4, y: 4, z: 4 (z_hi: 2, z_lo: 2; z = z_hi * 2 + z_lo), core: 2. Of those that a mesh axis runs over, the one named last changes fastest.
Arguments:
- e_field: float32 [3, 24, 1024, 2048], P(None, None, ('gx', 'gy'), 'gz'), may hold values from -6 to 6
- h_field: float32 [3, 24, 1024, 2048], P(None, None, ('gx', 'gy'), 'gz'), may hold values from -6 to 6
- material: int32 [24, 1024, 2048], P(None, ('gx', 'gy'), 'gz'), may hold values from 0 to 15
- decay_table: float32 [2, 16], replicated, may hold values from 0.6 to 1
- curl_table: float32 [2, 16], replicated, may hold values from 0.25 to 0.55
- residues: float32 [8, 16, 1024, 1024], P('gz', 'gy', 'gx'), may hold values from -0.046875 to 0.046875
- pole_decay: float32 [8, 16], P('gz', 'gy'), may hold values from 0.05 to 0.98
- pole_states: float32 [8, 16, 1024], P('gz', 'gy'), may hold values from -6 to 6
- direct: float32 [8, 1024], P('gz', 'gx'), may hold values from 0.2 to 1
- port_cell: int32 [8192], P(('gx', 'gy', 'gz')), may hold values from 0 to 393215
- port_owner: int32 [8192], P(('gx', 'gy', 'gz')), may hold values from 0 to 8191, each once
Outputs:
- e_out: float32 [3, 24, 1024, 2048], P(None, None, ('gx', 'gy'), 'gz')
- h_out: float32 [3, 24, 1024, 2048], P(None, None, ('gx', 'gy'), 'gz')
- states_out: float32 [8, 16, 1024], P('gz', 'gy')
Inputs may be any that keep to these rules, and one draw needn't show every extreme that they name: material ids index the tables. `port_cell`: a cell of the block of the device that holds the slot, numbered (i * 64 + j) * 256 + k; several slots may share a cell. `port_owner`: every port appears in exactly one slot.
All inputs are finite; a program needn't handle non-finite values.
Results may differ from a plain program's by a relative error of at most 0.0001.
Values sent between devices are 32-bit elements; how exact they have to be, the bound alone decides.
No kernel may reach another device: no remote copies, remote signals or barrier semaphores. Data moves between devices by JAX's collectives and lax.ppermute only.
A program may use at most 128 MiB of HBM per device.

v0:
```python
import jax
import jax.numpy as jnp
from jax import lax
from jax.sharding import PartitionSpec as P

STEPS = 2


def shifted(value, axis, steps):
    count = lax.axis_size(axis)
    initial, last = (max(0, -steps), min(count, count - steps))
    return lax.ppermute(value, axis, [(source, source + steps) for source in range(initial, last)])


def magnetic_update(electric, magnetic, ahead, decay, curl):
    first = decay * magnetic[0] - curl * (ahead[0] - electric[2] - (ahead[1] - electric[1]))
    second = decay * magnetic[1] - curl * (ahead[2] - electric[0] - (ahead[3] - electric[2]))
    third = decay * magnetic[2] - curl * (ahead[4] - electric[1] - (ahead[5] - electric[0]))
    return (first, second, third)


def electric_update(electric, magnetic, behind, decay, curl, source):
    first = decay * electric[0] + curl * (magnetic[2] - behind[0] - (magnetic[1] - behind[1]))
    second = decay * electric[1] + curl * (magnetic[0] - behind[2] - (magnetic[2] - behind[3]))
    third = decay * electric[2] + curl * (
        magnetic[1] - behind[4] - (magnetic[0] - behind[5]) - source
    )
    return (first, second, third)


def plane_y(face, offset):
    return shifted(face, ("gx", "gy"), offset)


def plane_z(face, offset):
    return shifted(face, "gz", offset)


def attach_after(field, plane, axis):
    inner = lax.slice_in_dim(field, 1, field.shape[axis], axis=axis)
    return jnp.concatenate([inner, jnp.expand_dims(plane, axis)], axis)


def attach_before(field, plane, axis):
    inner = lax.slice_in_dim(field, 0, field.shape[axis] - 1, axis=axis)
    return jnp.concatenate([jnp.expand_dims(plane, axis), inner], axis)


def shift_after(field, axis):
    return attach_after(
        field, jnp.zeros_like(lax.index_in_dim(field, 0, axis, keepdims=False)), axis
    )


def shift_before(field, axis):
    return attach_before(
        field, jnp.zeros_like(lax.index_in_dim(field, 0, axis, keepdims=False)), axis
    )


def body(
    e_field,
    h_field,
    material,
    decay_table,
    curl_table,
    residues,
    pole_decay,
    pole_states,
    direct,
    port_cell,
    port_owner,
):
    kinds = jnp.arange(decay_table.shape[1], dtype=jnp.int32)
    onehot = (material.reshape(1, -1) == kinds[:, None]).astype(jnp.float32)
    table = jnp.concatenate([decay_table, curl_table], 0)
    coefs = jnp.dot(table, onehot, precision=lax.Precision.HIGHEST).reshape((4,) + material.shape)
    decay_elec, decay_magn, curl_elec, curl_magn = (coefs[0], coefs[1], coefs[2], coefs[3])
    index_x = lax.axis_index("gx")
    index_y = lax.axis_index("gy")
    index_z = lax.axis_index("gz")
    count_z = lax.axis_size("gz")
    die_ports = pole_states.shape[2]
    row_count = residues.shape[2]
    total_ports = die_ports * count_z
    electric = (e_field[0], e_field[1], e_field[2])
    magnetic = (h_field[0], h_field[1], h_field[2])
    states = pole_states
    first_pole = (index_y == 0).astype(jnp.float32)
    for step in range(STEPS):
        sampled = electric[2].reshape(-1)[port_cell]
        volts_local = jnp.zeros((total_ports,), jnp.float32).at[port_owner].add(sampled)
        got_y = plane_y(jnp.stack([electric[0][:, 0], electric[2][:, 0]]), -1)
        got_z = plane_z(jnp.stack([electric[0][:, :, 0], electric[1][:, :, 0]]), -1)
        ahead = (
            attach_after(electric[2], got_y[1], 1),
            attach_after(electric[1], got_z[1], 2),
            attach_after(electric[0], got_z[0], 2),
            shift_after(electric[2], 0),
            shift_after(electric[1], 0),
            attach_after(electric[0], got_y[0], 1),
        )
        magnetic = magnetic_update(electric, magnetic, ahead, decay_magn, curl_magn)
        summed = lax.psum(volts_local, ("gx", "gy", "gz"))
        die_volts = lax.dynamic_slice_in_dim(summed, index_z * die_ports, die_ports)
        states = pole_decay[:, :, None] * states + die_volts[None, None, :]
        partial_value = jnp.einsum(
            "krc,kc->r", residues[0], states[0], precision=lax.Precision.HIGHEST
        )
        own_volts = lax.dynamic_slice_in_dim(die_volts, index_x * row_count, row_count)
        partial_value = partial_value + direct[0] * own_volts * first_pole
        dense = jnp.zeros((count_z, die_ports), jnp.float32)
        dense = lax.dynamic_update_slice(
            dense, partial_value[None, :], (index_z, index_x * row_count)
        )
        current = lax.psum(dense.reshape(-1), ("gx", "gy", "gz"))
        source = jnp.zeros((material.size,), jnp.float32).at[port_cell].add(current[port_owner])
        source = source.reshape(material.shape)
        got_y = plane_y(jnp.stack([magnetic[0][:, -1], magnetic[2][:, -1]]), 1)
        got_z = plane_z(jnp.stack([magnetic[0][:, :, -1], magnetic[1][:, :, -1]]), 1)
        behind = (
            attach_before(magnetic[2], got_y[1], 1),
            attach_before(magnetic[1], got_z[1], 2),
            attach_before(magnetic[0], got_z[0], 2),
            shift_before(magnetic[2], 0),
            shift_before(magnetic[1], 0),
            attach_before(magnetic[0], got_y[0], 1),
        )
        electric = electric_update(electric, magnetic, behind, decay_elec, curl_elec, source)
    return (jnp.stack(electric), jnp.stack(magnetic), states)


def solution(mesh):
    return jax.shard_map(
        body,
        mesh=mesh,
        in_specs=(
            P(None, None, ("gx", "gy"), "gz"),
            P(None, None, ("gx", "gy"), "gz"),
            P(None, ("gx", "gy"), "gz"),
            P(),
            P(),
            P("gz", "gy", "gx", None),
            P("gz", "gy"),
            P("gz", "gy", None),
            P("gz", "gx"),
            P(("gx", "gy", "gz")),
            P(("gx", "gy", "gz")),
        ),
        out_specs=(
            P(None, None, ("gx", "gy"), "gz"),
            P(None, None, ("gx", "gy"), "gz"),
            P("gz", "gy", None),
        ),
        check_vma=False,
    )
```

profile of v0, /device:TPU:7, one launch (start us, length us, event | category | flops | bytes accessed | tf_op | source)
XLA Modules:
  0.0 497.9 jit_solution(842361397629841166)
XLA Ops:
  0.6 2.8 fusion.67
  7.6 5.2 %collective-permute-start = (f32[2,24,256]{2,1,0:T(8,128)S(1)}, f32[2,24,256]{2,1,0:T(8,128)S(1)}, u32[]{:S(2)}, u32[]{:S(2)}) collective-permute-start(f32[2,24,256]{2,1,0:T(8,128)S(1)} %pad_maximum_fusion.2), channel_id=1, source_target_pairs={{8,0},{16,8},{24,16},{32,24},{40,32},{48,40},{56,48},{64,56},{72,6... | collective-permute-start | bytes 147464 | tf_op jit(solution)/shard_map/ppermute | solution.py:12
  23.7 4.0 fusion.65
  28.5 7.9 %fusion = f32[4,393216]{1,0:T(4,128)S(1)} fusion(s32[393216]{0:T(1024)S(1)} %bitcast.171, f32[2,16]{1,0:T(2,128)S(1)} %copy-done.27, f32[2,16]{1,0:T(2,128)S(1)} %copy-done.28), kind=kOutput, calls=%fused_computation.9 | convolution fusion | flops 308281408 | bytes 7864576 | tf_op jit(solution)/shard_map/dot_general | solution.py:77
  36.4 19.6 %slice_reduce_fusion.2 = (f32[393216]{0:T(1024)}, f32[393216]{0:T(1024)}, f32[393216]{0:T(1024)}, f32[393216]{0:T(1024)}) fusion(f32[4,393216]{1,0:T(4,128)S(1)} %fusion), kind=kLoop, calls=%fused_computation.19 | loop fusion | bytes 12582912 | tf_op jit(solution)/shard_map/slice | solution.py:78
  56.0 4.7 fusion.66
  65.3 66.0 %psum.28 = f32[8192]{0:T(1024)S(1)} all-reduce(f32[8192]{0:T(1024)S(1)} %scatter_custom_fusion), channel_id=1, replica_groups=mesh['gx'=4,'gy'=4,'gz'=8] {'gx','gy','gz'}, use_global_device_ids=true, to_apply=%region_1.0 | all-reduce | flops 8192 | bytes 65536 | tf_op jit(solution)/shard_map/psum | solution.py:104
  131.4 5.4 %copy_bitcast_fusion = (f32[23,64,256]{2,0,1:T(8,128)}, f32[23,64,256]{2,0,1:T(8,128)}) fusion(f32[1,23,64,256]{3,2,1,0:T(8,128)} %get-tuple-element.40, f32[1,23,64,256]{3,2,1,0:T(8,128)} %get-tuple-element.41), kind=kLoop, calls=%fused_computation.78 | loop fusion | bytes 6029312 | tf_op jit(solution)/shard_map/slice | solution.py:40
  136.9 3.3 fusion.4
  149.2 64.1 %psum.29 = f32[8192]{0:T(1024)S(1)} all-reduce(f32[8192]{0:T(1024)S(1)} %bitcast.180), channel_id=1, replica_groups=mesh['gx'=4,'gy'=4,'gz'=8] {'gx','gy','gz'}, use_global_device_ids=true, to_apply=%region_2.0 | all-reduce | flops 8192 | bytes 65536 | tf_op jit(solution)/shard_map/psum | solution.py:116
  222.8 18.8 %fusion.17 = (f32[24,64,256]{2,0,1:T(8,128)S(1)}, f32[24,64,256]{2,0,1:T(8,128)S(1)}, f32[24,64,256]{2,0,1:T(8,128)S(1)}) fusion(f32[24,64,1]{2,0,1:T(8,128)} %copy.468, f32[24,64,255]{2,0,1:T(8,128)} %slice.304, f32[1,24,64,256]{3,2,1,0:T(8,128)} %get-tuple-element.42, f32[23,64,256]{2,0,1:T(8,128)} %get-tuple-element.64, f32[24,64,256]{2,1,0:T(8,128)} %squeeze.49, ...), kind=kLoop, calls=%fused_computation.37 | loop fusion | flops 8650752 | bytes 26607616 | tf_op jit(solution)/shard_map/sub | solution.py:17
  247.2 3.5 collective-permute-start.3
  253.3 3.1 collective-permute-start.2
  259.9 15.1 %fusion.20 = (f32[24,64,256]{2,0,1:T(8,128)S(1)}, f32[24,64,256]{2,0,1:T(8,128)S(1)}, f32[24,64,256]{2,0,1:T(8,128)S(1)}) fusion(f32[24,64,256]{2,0,1:T(8,128)} %copy-done.3, f32[24,64,255]{2,0,1:T(8,128)} %bitcast.158, f32[24,64,1]{2,0,1:T(8,128)} %copy.478, f32[24,64,256]{2,0,1:T(8,128)} %copy-done.6, f32[23,64,256]{2,0,1:T(8,128)} %bitcast.161, ...), kind=kLoop, calls=%fused_computation.42 | loop fusion | flops 9043968 | bytes 28180480 | tf_op jit(solution)/shard_map/add | solution.py:24
  290.6 65.0 %psum.30 = f32[8192]{0:T(1024)S(1)} all-reduce(f32[8192]{0:T(1024)S(1)} %scatter_custom_fusion.2), channel_id=1, replica_groups=mesh['gx'=4,'gy'=4,'gz'=8] {'gx','gy','gz'}, use_global_device_ids=true, to_apply=%region_5.0 | all-reduce | flops 8192 | bytes 65536 | tf_op jit(solution)/shard_map/psum | solution.py:104
  356.4 2.8 collective-permute-start.4
  362.0 3.5 collective-permute-start.5
  365.5 5.5 %fusion.2 = f32[1,256,1]{1,0,2:T(1,128)S(1)} fusion(f32[1,4,256,1024]{3,2,1,0:T(8,128)} %param.16, f32[4,1024,1]{1,0,2:T(4,128)S(1)} %fusion.68), kind=kOutput, calls=%fused_computation.13 | convolution fusion | flops 12582912 | bytes 4211712 | tf_op jit(solution)/shard_map/krc,kc->r/dot_general | solution.py:107
  371.4 64.9 %psum.31 = f32[8192]{0:T(1024)S(1)} all-reduce(f32[8192]{0:T(1024)S(1)} %bitcast.181), channel_id=1, replica_groups=mesh['gx'=4,'gy'=4,'gz'=8] {'gx','gy','gz'}, use_global_device_ids=true, to_apply=%region_6.0 | all-reduce | flops 8192 | bytes 65536 | tf_op jit(solution)/shard_map/psum | solution.py:116
  444.3 10.0 %fusion.37 = (f32[24,64,256]{2,0,1:T(8,128)}, f32[24,64,256]{2,0,1:T(8,128)S(1)}, f32[24,64,256]{2,0,1:T(8,128)}) fusion(f32[24,64,256]{2,0,1:T(8,128)} %copy-done.1, f32[24,64,1]{2,0,1:T(8,128)} %copy.491, f32[24,64,255]{2,0,1:T(8,128)} %slice.331, f32[24,64,256]{2,0,1:T(8,128)S(1)} %get-tuple-element.36, f32[23,64,256]{2,0,1:T(8,128)} %slice.333, ...), kind=kLoop, calls=%fused_computation.65 | loop fusion | flops 8650752 | bytes 26607616 | tf_op jit(solution)/shard_map/sub | solution.py:17
  459.7 5.6 %collective-permute-start.7 = (f32[2,24,64]{2,1,0:T(8,128)S(1)}, f32[2,24,64]{2,1,0:T(8,128)S(1)}, u32[]{:S(2)}, u32[]{:S(2)}) collective-permute-start(f32[2,24,64]{2,1,0:T(8,128)S(1)} %pad_maximum_fusion.9), channel_id=1, source_target_pairs={{0,1},{1,2},{2,3},{3,4},{4,5},{5,6},{6,7},{8,9},{9,10},{10,11},{11... | collective-permute-start | bytes 36872 | tf_op jit(solution)/shard_map/ppermute | solution.py:12
  471.7 3.6 copy.505
  481.9 11.9 %fusion.34 = (f32[1,24,64,256]{3,1,2,0:T(8,128)S(1)}, f32[1,24,64,256]{3,1,2,0:T(8,128)S(1)}, f32[1,24,64,256]{3,1,2,0:T(8,128)S(1)}) fusion(f32[24,64,256]{2,0,1:T(8,128)} %get-tuple-element.33, f32[24,63,256]{2,0,1:T(8,128)} %slice.330, f32[24,1,256]{2,0,1:T(8,128)S(1)} %get-tuple-element.48, f32[24,64,256]{2,0,1:T(8,128)S(1)} %copy-done, ...), kind=kLoop, calls=%fused_computation.61 | loop fusion | flops 9043968 | bytes 28180480 | tf_op jit(solution)/shard_map/stack | solution.py:130
  494.2 3.6 copy.504
  (173 shorter events, 96.6 us)
Async XLA Ops:
  3.4 11.7 %copy-start.10 = (f32[1,24,64,256]{3,2,1,0:T(8,128)}, f32[1,24,64,256]{3,2,1,0:T(8,128)S(1)}, u32[]{:S(2)}) copy-start(f32[1,24,64,256]{3,2,1,0:T(8,128)S(1)} %get-tuple-element.45) | copy-start | bytes 4718596
  3.4 57.3 %copy-start.9 = (f32[1,24,64,256]{3,2,1,0:T(8,128)}, f32[1,24,64,256]{3,2,1,0:T(8,128)S(1)}, u32[]{:S(2)}) copy-start(f32[1,24,64,256]{3,2,1,0:T(8,128)S(1)} %get-tuple-element.46) | copy-start | bytes 4718596
  5.5 7.3 %copy-start.12 = (f32[1,24,64,256]{3,1,2,0:T(8,128)}, f32[1,24,64,256]{3,1,2,0:T(8,128)S(1)}, u32[]{:S(2)}) copy-start(f32[1,24,64,256]{3,1,2,0:T(8,128)S(1)} %copy.593) | copy-start | bytes 4718596
  7.6 215.2 %collective-permute-start = (f32[2,24,256]{2,1,0:T(8,128)S(1)}, f32[2,24,256]{2,1,0:T(8,128)S(1)}, u32[]{:S(2)}, u32[]{:S(2)}) collective-permute-start(f32[2,24,256]{2,1,0:T(8,128)S(1)} %pad_maximum_fusion.2), channel_id=1, source_target_pairs={{8,0},{16,8},{24,16},{32,24},{40,32},{48,40},{56,48},{64,56},{72,6... | collective-permute-start | bytes 147464 | tf_op jit(solution)/shard_map/ppermute | solution.py:12
  16.1 6.0 %copy-start.13 = (f32[1,24,64,256]{3,1,2,0:T(8,128)S(1)}, f32[1,24,64,256]{3,1,2,0:T(8,128)}, u32[]{:S(2)}) copy-start(f32[1,24,64,256]{3,1,2,0:T(8,128)} %copy-done.12) | copy-start | bytes 4718596
  19.6 200.6 %collective-permute-start.1 = (f32[2,24,64]{2,1,0:T(8,128)S(1)}, f32[2,24,64]{2,1,0:T(8,128)S(1)}, u32[]{:S(2)}, u32[]{:S(2)}) collective-permute-start(f32[2,24,64]{2,1,0:T(8,128)S(1)} %pad_maximum_fusion.6), channel_id=1, source_target_pairs={{1,0},{2,1},{3,2},{4,3},{5,4},{6,5},{7,6},{9,8},{10,9},{11,10},{12... | collective-permute-start | bytes 36872 | tf_op jit(solution)/shard_map/ppermute | solution.py:12
  23.7 4.0 copy-start.23
  131.4 5.4 %copy-start.24 = (f32[1,4,1024]{2,1,0:T(4,128)S(1)}, f32[1,4,1024]{2,1,0:T(4,128)}, u32[]{:S(2)}) copy-start(f32[1,4,1024]{2,1,0:T(4,128)} %param.18) | copy-start | bytes 49156
  131.4 5.4 %copy-start.25 = (f32[1,4]{1,0:T(1,128)S(1)}, f32[1,4]{1,0:T(1,128)}, u32[]{:S(2)}) copy-start(f32[1,4]{1,0:T(1,128)} %param.17) | copy-start | bytes 52
  131.4 5.5 %copy-start.14 = (f32[1,4,256,1024]{3,2,1,0:T(8,128)S(1)}, f32[1,4,256,1024]{3,2,1,0:T(8,128)}, u32[]{:S(2)}) copy-start(f32[1,4,256,1024]{3,2,1,0:T(8,128)} %param.16) | copy-start | bytes 12582916
  136.9 3.4 copy-start.26
  140.2 2.0 copy-start.18
  241.6 9.1 %copy-start.3 = (f32[24,64,256]{2,0,1:T(8,128)}, f32[24,64,256]{2,0,1:T(8,128)S(1)}, u32[]{:S(2)}) copy-start(f32[24,64,256]{2,0,1:T(8,128)S(1)} %get-tuple-element.38) | copy-start | bytes 4718596
  247.2 4.8 copy-start.7
  247.2 9.2 %collective-permute-start.3 = (f32[2,24,64]{2,1,0:T(8,128)S(1)}, f32[2,24,64]{2,1,0:T(8,128)S(1)}, u32[]{:S(2)}, u32[]{:S(2)}) collective-permute-start(f32[2,24,64]{2,1,0:T(8,128)S(1)} %pad_maximum_fusion.7), channel_id=1, source_target_pairs={{0,1},{1,2},{2,3},{3,4},{4,5},{5,6},{6,7},{8,9},{9,10},{10,11},{11... | collective-permute-start | bytes 36872 | tf_op jit(solution)/shard_map/ppermute | solution.py:12
  253.3 6.6 %collective-permute-start.2 = (f32[2,24,256]{2,1,0:T(8,128)S(1)}, f32[2,24,256]{2,1,0:T(8,128)S(1)}, u32[]{:S(2)}, u32[]{:S(2)}) collective-permute-start(f32[2,24,256]{2,1,0:T(8,128)S(1)} %pad_maximum_fusion.3), channel_id=1, source_target_pairs={{0,8},{8,16},{16,24},{24,32},{32,40},{40,48},{48,56},{56,64},{64,7... | collective-permute-start | bytes 147464 | tf_op jit(solution)/shard_map/ppermute | solution.py:12
  275.0 3.5 copy-start.2
  275.0 8.0 %copy-start.1 = (f32[24,64,256]{2,0,1:T(8,128)}, f32[24,64,256]{2,0,1:T(8,128)S(1)}, u32[]{:S(2)}) copy-start(f32[24,64,256]{2,0,1:T(8,128)S(1)} %get-tuple-element.35) | copy-start | bytes 4718596
  356.4 87.9 %collective-permute-start.4 = (f32[2,24,256]{2,1,0:T(8,128)S(1)}, f32[2,24,256]{2,1,0:T(8,128)S(1)}, u32[]{:S(2)}, u32[]{:S(2)}) collective-permute-start(f32[2,24,256]{2,1,0:T(8,128)S(1)} %pad_maximum_fusion.4), channel_id=1, source_target_pairs={{8,0},{16,8},{24,16},{32,24},{40,32},{48,40},{56,48},{64,56},{72,6... | collective-permute-start | bytes 147464 | tf_op jit(solution)/shard_map/ppermute | solution.py:12
  362.0 79.8 %collective-permute-start.5 = (f32[2,24,64]{2,1,0:T(8,128)S(1)}, f32[2,24,64]{2,1,0:T(8,128)S(1)}, u32[]{:S(2)}, u32[]{:S(2)}) collective-permute-start(f32[2,24,64]{2,1,0:T(8,128)S(1)} %pad_maximum_fusion.8), channel_id=1, source_target_pairs={{1,0},{2,1},{3,2},{4,3},{5,4},{6,5},{7,6},{9,8},{10,9},{11,10},{12... | collective-permute-start | bytes 36872 | tf_op jit(solution)/shard_map/ppermute | solution.py:12
  454.3 2.8 copy-start
  459.7 17.7 %collective-permute-start.7 = (f32[2,24,64]{2,1,0:T(8,128)S(1)}, f32[2,24,64]{2,1,0:T(8,128)S(1)}, u32[]{:S(2)}, u32[]{:S(2)}) collective-permute-start(f32[2,24,64]{2,1,0:T(8,128)S(1)} %pad_maximum_fusion.9), channel_id=1, source_target_pairs={{0,1},{1,2},{2,3},{3,4},{4,5},{5,6},{6,7},{8,9},{9,10},{10,11},{11... | collective-permute-start | bytes 36872 | tf_op jit(solution)/shard_map/ppermute | solution.py:12
  466.1 2.4 copy-start.8
  475.3 6.6 %collective-permute-start.6 = (f32[2,24,256]{2,1,0:T(8,128)S(1)}, f32[2,24,256]{2,1,0:T(8,128)S(1)}, u32[]{:S(2)}, u32[]{:S(2)}) collective-permute-start(f32[2,24,256]{2,1,0:T(8,128)S(1)} %pad_maximum_fusion.5), channel_id=1, source_target_pairs={{0,8},{8,16},{16,24},{24,32},{32,40},{40,48},{48,56},{56,64},{64,7... | collective-permute-start | bytes 147464 | tf_op jit(solution)/shard_map/ppermute | solution.py:12
  (15 other events, 22.4 us)
where the time goes:
time: 503 us; the launch traced here: 498 us
  blocking collectives  260 us (52%)
  local copies, waits for them, and re-layouts  124 us (25%)
  other arithmetic  64.9 us (13%)
  starting transfers between devices  28.2 us (6%)
  matrix products  16.7 us (3%)
    psum x2, blocking collectives, body(): summed = lax.psum(volts_local, ('gx', 'gy', 'gz'))  131 us
    psum x2, blocking collectives, body(): current = lax.psum(dense.reshape(-1), ('gx', 'gy', 'gz'))  129 us
    sub x2, other arithmetic, magnetic_update(): decay * magnetic[1]  28.8 us
    ppermute x8, starting transfers between devices, shifted(): lax.ppermute(value, axis, [(source, source + steps) for source in range(i...  28.2 us
    slice x12, local copies, waits for them, and re-layouts, attach_after(): inner = lax.slice_in_dim(field, 1, field.shape[axis], axis=axis)  23.4 us
    unnamed x72, local copies, waits for them, and re-layouts  20.4 us
    slice x1, local copies, waits for them, and re-layouts, body(): coefs[2]  19.6 us
    add x1, other arithmetic, electric_update(): decay * electric[1]  15.1 us
  transfers between devices with their start and end apart: 8, of which 2 were waited for; matrix products, arithmetic and copies ran while one was open for 22% of the time, Pallas kernels for 0%

commit v1 on v0

v1 whole, which is shorter than its diff:
```python
import jax
import jax.numpy as jnp
from jax import lax
from jax.experimental import pallas as pl
from jax.experimental.pallas import tpu as pltpu
from jax.sharding import PartitionSpec as P

ALL = ("gx", "gy", "gz")
F32 = jnp.float32
I32 = jnp.int32
LANES = 128
VMEM = pl.BlockSpec(memory_space=pltpu.VMEM)
SMEM = pl.BlockSpec(memory_space=pltpu.SMEM)
ANY = pl.BlockSpec(memory_space=pl.ANY)


def call(kernel, outs, ins, scratch=(), aliases=None, limit=16, specs_out=None):
    return pl.pallas_call(
        kernel,
        out_shape=tuple(jax.ShapeDtypeStruct(s, d) for s, d in outs),
        in_specs=list(ins),
        out_specs=tuple(specs_out) if specs_out else tuple(VMEM for _ in outs),
        scratch_shapes=list(scratch),
        input_output_aliases=aliases or {},
        compiler_params=pltpu.CompilerParams(vmem_limit_bytes=limit * 2**20),
    )


def shifted(value, axis, steps):
    count = lax.axis_size(axis)
    initial, last = (max(0, -steps), min(count, count - steps))
    return lax.ppermute(value, axis, [(source, source + steps) for source in range(initial, last)])


def lane_iota(shape):
    return lax.broadcasted_iota(I32, shape, len(shape) - 1)


def row_iota(shape):
    return lax.broadcasted_iota(I32, shape, 0)


def lookup(row, index):
    return jnp.take_along_axis(
        jnp.broadcast_to(row, index.shape), index, axis=1, mode="promise_in_bounds"
    )


def table_lookup(row, index):
    half = index.shape[1] // 2
    return jnp.concatenate([lookup(row, index[:, :half]), lookup(row, index[:, half:])], 1)


def load_tables(scratch, decay_ref, curl_ref):
    scratch[...] = jnp.zeros_like(scratch)
    scratch[0:2, 0:16] = decay_ref[...]
    scratch[2:4, 0:16] = curl_ref[...]


def cell_of(cell):
    return cell >> 14, (cell >> 8) & 63, cell & 255


def sample_rows(read_row, cell_ref, count):
    lane = lane_iota((1, LANES))

    def step(slot, acc):
        i, y, k = cell_of(cell_ref[slot])
        row = read_row(i, y)
        half = jnp.where(k >= LANES, row[:, LANES:], row[:, :LANES])
        moved = pltpu.roll(half, (slot - k) & (LANES - 1), 1)
        return jnp.where(lane == slot, moved, acc)

    return lax.fori_loop(0, count, step, jnp.zeros((1, LANES), F32), unroll=8)


def add_sources(field_ref, comp, cell_ref, values, count):
    lane = lane_iota((1, 2 * LANES))
    wide = jnp.broadcast_to(values, (8, LANES))

    def step(slot, carry):
        i, y, k = cell_of(cell_ref[slot])
        splat = lookup(wide[0:1], jnp.full((8, LANES), slot, I32))[0:1]
        both = jnp.concatenate([splat, splat], 1)
        row = field_ref[comp, i, pl.ds(y, 1), :]
        field_ref[comp, i, pl.ds(y, 1), :] = row - jnp.where(lane == k, both, 0.0)
        return carry

    lax.fori_loop(0, count, step, 0, unroll=4)


def electric_edges(e_ref, y_out, z_out):
    nx, ny = e_ref.shape[1], e_ref.shape[2]
    lane = lane_iota((ny, LANES))

    def step(i, acc):
        y_out[pl.ds(i, 1), :] = e_ref[0, i, 0:1, :]
        y_out[pl.ds(nx + i, 1), :] = e_ref[2, i, 0:1, :]
        for c in range(2):
            j = c * nx + i
            acc = jnp.where(lane == j, pltpu.roll(e_ref[c, i, :, 0:LANES], j, 1), acc)
        return acc

    z_out[...] = lax.fori_loop(0, nx, step, jnp.zeros((ny, LANES), F32))


def h_kernel(e_ref, h_ref, mat_ref, decay_ref, curl_ref, yh_ref, zh_ref, out_ref, yl_ref, zl_ref, tab):
    load_tables(tab, decay_ref, curl_ref)
    nx, ny, nz = mat_ref.shape
    row = row_iota((ny, nz))
    lane = lane_iota((ny, LANES))

    def from_y(value, halo):
        return jnp.where(row == ny - 1, halo, pltpu.roll(value, ny - 1, 0))

    def from_z(value, j):
        moved = pltpu.roll(value, nz - 1, 1)
        halo = pltpu.roll(zh_ref[...], (LANES - 1 - j) & (LANES - 1), 1)
        right = jnp.where(lane == LANES - 1, halo, moved[:, nz - LANES :])
        return jnp.concatenate([moved[:, : nz - LANES], right], 1)

    def step(i, acc):
        mat = mat_ref[i]
        decay = table_lookup(tab[1:2, :], mat)
        curl = table_lookup(tab[3:4, :], mat)
        ex, ey, ez = e_ref[0, i], e_ref[1, i], e_ref[2, i]
        after = jnp.minimum(i + 1, nx - 1)
        inside = i < nx - 1
        ey_x = jnp.where(inside, e_ref[1, after], 0.0)
        ez_x = jnp.where(inside, e_ref[2, after], 0.0)
        hx = decay * h_ref[0, i] - curl * (
            (from_y(ez, yh_ref[pl.ds(nx + i, 1), :]) - ez) - (from_z(ey, nx + i) - ey)
        )
        hy = decay * h_ref[1, i] - curl * ((from_z(ex, i) - ex) - (ez_x - ez))
        hz = decay * h_ref[2, i] - curl * (
            (ey_x - ey) - (from_y(ex, yh_ref[pl.ds(i, 1), :]) - ex)
        )
        out_ref[0, i] = hx
        out_ref[1, i] = hy
        out_ref[2, i] = hz
        yl_ref[pl.ds(i, 1), :] = hx[ny - 1 : ny, :]
        yl_ref[pl.ds(nx + i, 1), :] = hz[ny - 1 : ny, :]
        for c, value in enumerate((hx, hy)):
            j = c * nx + i
            moved = pltpu.roll(value[:, nz - LANES :], (j + 1) & (LANES - 1), 1)
            acc = jnp.where(lane == j, moved, acc)
        return acc

    zl_ref[...] = lax.fori_loop(0, nx, step, jnp.zeros((ny, LANES), F32))


def e_slab(i, e_ref, h_ref, mat_ref, yl_ref, zl_ref, tab):
    nx, ny, nz = mat_ref.shape
    row = row_iota((ny, nz))
    lane = lane_iota((ny, LANES))

    def from_y(value, halo):
        return jnp.where(row == 0, halo, pltpu.roll(value, 1, 0))

    def from_z(value, j):
        moved = pltpu.roll(value, 1, 1)
        halo = pltpu.roll(zl_ref[...], (LANES - j) & (LANES - 1), 1)
        left = jnp.where(lane == 0, halo, moved[:, :LANES])
        return jnp.concatenate([left, moved[:, LANES:]], 1)

    mat = mat_ref[i]
    decay = table_lookup(tab[0:1, :], mat)
    curl = table_lookup(tab[2:3, :], mat)
    hx, hy, hz = h_ref[0, i], h_ref[1, i], h_ref[2, i]
    before = jnp.maximum(i - 1, 0)
    inside = i > 0
    hy_x = jnp.where(inside, h_ref[1, before], 0.0)
    hz_x = jnp.where(inside, h_ref[2, before], 0.0)
    ex = decay * e_ref[0, i] + curl * (
        (hz - from_y(hz, yl_ref[pl.ds(nx + i, 1), :])) - (hy - from_z(hy, nx + i))
    )
    ey = decay * e_ref[1, i] + curl * ((hx - from_z(hx, i)) - (hz - hz_x))
    ez = decay * e_ref[2, i] + curl * (
        (hy - hy_x) - (hx - from_y(hx, yl_ref[pl.ds(i, 1), :]))
    )
    return ex, ey, ez


def e_kernel(e_ref, h_ref, mat_ref, decay_ref, curl_ref, yl_ref, zl_ref, cell_ref, out_ref, got_ref, tab):
    load_tables(tab, decay_ref, curl_ref)

    def step(i, carry):
        ex, ey, ez = e_slab(i, e_ref, h_ref, mat_ref, yl_ref, zl_ref, tab)
        out_ref[0, i] = ex
        out_ref[1, i] = ey
        out_ref[2, i] = ez
        return carry

    lax.fori_loop(0, mat_ref.shape[0], step, 0)
    got_ref[...] = sample_rows(
        lambda i, y: out_ref[2, i, pl.ds(y, 1), :], cell_ref, cell_ref.shape[0]
    )


def e_last_kernel(
    e_ref, h_ref, mat_ref, decay_ref, curl_ref, yl_ref, zl_ref, e_out, h_out, ez_ref, tab, buf, sem, h_sem
):
    load_tables(tab, decay_ref, curl_ref)
    nx = mat_ref.shape[0]
    h_copy = pltpu.make_async_copy(h_ref, h_out, h_sem)
    h_copy.start()

    def out_copy(i, c):
        return pltpu.make_async_copy(buf.at[c, i], e_out.at[c, i], sem.at[c])

    def step(i, carry):
        ex, ey, ez = e_slab(i, e_ref, h_ref, mat_ref, yl_ref, zl_ref, tab)
        buf[0, i] = ex
        buf[1, i] = ey
        ez_ref[i] = ez
        out_copy(i, 0).start()
        out_copy(i, 1).start()
        return carry

    lax.fori_loop(0, nx, step, 0)
    for c in range(2):
        pltpu.make_async_copy(buf.at[c], e_out.at[c], sem.at[c]).wait()
    h_copy.wait()


def finish_kernel(e_in, ez_ref, got_ref, curl_ref, cell_ref, e_out, work, sem):
    del e_in
    count = cell_ref.shape[0]
    work[0] = ez_ref[...]
    values = jnp.sum(got_ref[...], 0, keepdims=True) * curl_ref[...]
    add_sources(work, 0, cell_ref, values, count)
    copy = pltpu.make_async_copy(work.at[0], e_out.at[2], sem)
    copy.start()
    copy.wait()


def sample_kernel(e_ref, cell_ref, owner_ref, send_ref, y_out, z_out):
    count = cell_ref.shape[0]
    got = sample_rows(lambda i, y: e_ref[2, i, pl.ds(y, 1), :], cell_ref, count)
    owner = owner_ref[...].astype(F32)
    line = jnp.concatenate([got[:, :count], owner], 1)
    send_ref[...] = jnp.broadcast_to(line, send_ref.shape)
    electric_edges(e_ref, y_out, z_out)


def slot_kernel(mat_ref, curl_ref, cell_ref, cells_ref, line_ref, tab):
    count = cell_ref.shape[0]
    tab[...] = jnp.zeros_like(tab)
    tab[0:1, 0:16] = curl_ref[0:1, :]
    kinds = sample_rows(
        lambda i, y: mat_ref[i, pl.ds(y, 1), :].astype(F32), cell_ref, count
    )
    curl = lookup(tab[0:1, :], jnp.broadcast_to(kinds, (8, LANES)).astype(I32))[0:1]
    cells = cells_ref[...]
    cells = jnp.concatenate([cells, cells], 1)
    twin = jnp.zeros((1, LANES), F32)
    for r in range(1, count):
        twin = jnp.where(pltpu.roll(cells, r, 1) == cells, 1.0, twin)
    lane = lane_iota((1, LANES))
    line_ref[0:1, :] = jnp.where(lane < count, curl, 0.0)
    line_ref[1:2, :] = jnp.where(lane < count, cells.astype(F32), twin)


def across(value):
    return jnp.concatenate(
        [jnp.sum(value[h : h + LANES].T, 0, keepdims=True) for h in (0, LANES)], 1
    )


def residue_kernel(res_ref, decay_ref, state_ref, sum_ref, damp_ref, base_ref, line, acc):
    poles, rows, ports = res_ref.shape[1:]
    tiles = ports // LANES
    for k in range(poles):
        line[k : k + 1, :] = decay_ref[0, k] * state_ref[0, k : k + 1, :]
        line[poles + k : poles + k + 1, :] = decay_ref[0, k] * line[k : k + 1, :]

    def step(block, carry):
        at = pl.ds(pl.multiple_of(block * 8, 8), 8)
        one = jnp.zeros((8, LANES), F32)
        two = jnp.zeros((8, LANES), F32)
        for t in range(tiles):
            lanes = slice(t * LANES, (t + 1) * LANES)
            total = damp = None
            for k in range(poles):
                value = res_ref[0, k, at, lanes]
                one = one + value * line[k : k + 1, lanes]
                two = two + value * line[poles + k : poles + k + 1, lanes]
                scaled = decay_ref[0, k] * value
                total = value if total is None else total + value
                damp = scaled if damp is None else damp + scaled
            sum_ref[at, lanes] = total
            damp_ref[at, lanes] = damp
        acc[0, at, :] = one
        acc[1, at, :] = two
        return carry

    lax.fori_loop(0, rows // 8, step, 0)
    base_ref[0:1, :] = across(acc[0])
    base_ref[1:2, :] = across(acc[1])


def apply(mat_ref, volts):
    total = None
    for t in range(volts.shape[0]):
        part = mat_ref[:, t * LANES : (t + 1) * LANES] * volts[t : t + 1, :]
        total = part if total is None else total + part
    return total


def fetch(tab_ref, rows, lanes):
    acc = jnp.zeros(lanes.shape, F32)
    for r in range(tab_ref.shape[0]):
        acc = jnp.where(rows == r, lookup(tab_ref[r : r + 1, :], lanes), acc)
    return acc


def own_ports(volts_ref, index_x):
    return jnp.concatenate(
        [volts_ref[pl.ds(2 * index_x + h, 1), :] for h in range(2)], 1
    )


def first_kernel(recv_ref, sum_ref, base_ref, direct_ref, where_ref, own_ref, at_ref, volts_ref, cur_ref, tab):
    index_x, index_y, die = where_ref[0], where_ref[1], where_ref[2]
    half = lane_iota((64, LANES)) < 64
    even = recv_ref[pl.ds(0, 64, stride=2), :]
    odd = recv_ref[pl.ds(1, 64, stride=2), :]
    tab[...] = jnp.where(half, even, pltpu.roll(odd, 64, 1))
    owner = jnp.where(half, pltpu.roll(even, 64, 1), odd).astype(I32)
    own_ref[...] = owner
    high, low = owner >> 7, owner & (LANES - 1)
    port = die * 8 + row_iota((8, LANES))
    lane = lane_iota((8, LANES)).astype(F32)
    spot = row_iota((LANES, LANES))
    found = jnp.zeros((16, LANES), F32)
    for r in range(0, 64, 2):
        picks, marks = [], []
        for q in (r, r + 1):
            mine = high[q : q + 1, :] == port
            picks.append(
                jnp.concatenate(
                    [jnp.where(mine, float(q), 0.0), jnp.where(mine, lane, 0.0)], 0
                ).astype(jnp.bfloat16)
            )
            marks.append(
                jnp.where(low[q : q + 1, :] == spot, 1.0, 0.0).astype(jnp.bfloat16)
            )
        found = found + lax.dot_general(
            jnp.concatenate(picks, 1),
            jnp.concatenate(marks, 1),
            (((1,), (1,)), ((), ())),
            preferred_element_type=F32,
        )
    found = found.astype(I32)
    rows, lanes = found[0:8], found[8:16]
    at_ref[0] = rows
    at_ref[1] = lanes
    volts = fetch(tab, rows, lanes)
    volts_ref[...] = volts
    current = across(apply(sum_ref, volts)) + base_ref[0:1, :]
    through = direct_ref[...] * own_ports(volts_ref, index_x)
    cur_ref[...] = current + jnp.where(index_y == 0, through, 0.0)


def pack_kernel(got_ref, line_ref, cur_ref, send_ref):
    lane = lane_iota((1, LANES))
    first = jnp.where(lane < 64, got_ref[...], pltpu.roll(line_ref[0:1, :], 64, 1))
    shape = (8, LANES)
    turn = row_iota(shape) & 3
    block = jnp.where(turn == 0, first, jnp.where(turn == 3, line_ref[1:2, :], 0.0))
    block = jnp.where(turn == 1, cur_ref[:, :LANES], block)
    block = jnp.where(turn == 2, cur_ref[:, LANES:], block)

    def step(n, carry):
        send_ref[pl.ds(pl.multiple_of(n * 8, 8), 8), :] = block
        return carry

    lax.fori_loop(0, send_ref.shape[0] // 8, step, 0, unroll=8)


def turn64(value, r):
    lane = lane_iota(value.shape) & 63
    return jnp.where(
        lane >= r, pltpu.roll(value, r, 1), pltpu.roll(value, (r + 64) & (LANES - 1), 1)
    )


def second_kernel(
    recv_ref, own_ref, at_ref, volts_ref, sum_ref, damp_ref, base_ref, direct_ref,
    decay_ref, state_ref, owner_ref, where_ref,
    states_ref, send_ref, mine_ref,
    cur_tab, ez_tab, curl_tab, shared, next_ref,
):
    index_x, index_y, die = where_ref[0], where_ref[1], where_ref[2]
    half = lane_iota((64, LANES)) < 64
    for gx in range(4):
        for h in range(2):
            total = None
            for gy in range(4):
                part = recv_ref[pl.ds((gx * 4 + gy) * 32 + 1 + h, 8, stride=4), :]
                total = part if total is None else total + part
            cur_tab[pl.ds(gx * 2 + h, 8, stride=8), :] = total
    even = recv_ref[pl.ds(0, 64, stride=8), :]
    odd = recv_ref[pl.ds(4, 64, stride=8), :]
    ez_tab[...] = jnp.where(half, even, pltpu.roll(odd, 64, 1))
    curl_tab[...] = jnp.where(half, pltpu.roll(even, 64, 1), odd)
    rows, lanes = at_ref[0], at_ref[1]
    shared[0:8, :] = cur_tab[pl.ds(pl.multiple_of(die * 8, 8), 8), :]

    even = recv_ref[pl.ds(3, 64, stride=8), :]
    odd = recv_ref[pl.ds(7, 64, stride=8), :]
    flags = jnp.where(half, 0.0, jnp.maximum(even, odd))

    @pl.when(jnp.max(flags) > 0.5)
    def _():
        cells = jnp.where(half, even, pltpu.roll(odd, 64, 1))
        owner = own_ref[...]
        high, low = owner >> 7, owner & (LANES - 1)

        def pick(r, acc):
            return jnp.where(high == r, lookup(cur_tab[pl.ds(r, 1), :], low), acc)

        slots = lax.fori_loop(0, 64, pick, jnp.zeros((64, LANES), F32))

        def gather(r, acc):
            same = turn64(cells, r) == cells
            return acc + jnp.where(same, turn64(slots, r), 0.0)

        shared[8:72, :] = lax.fori_loop(1, 64, gather, slots)
        shared[0:8, :] = fetch(shared.at[8:72], rows, lanes)

    volts = fetch(ez_tab, rows, lanes) - fetch(curl_tab, rows, lanes) * shared[0:8, :]
    next_ref[...] = volts
    current = across(apply(sum_ref, volts) + apply(damp_ref, volts_ref[...])) + base_ref[1:2, :]
    through = direct_ref[...] * own_ports(next_ref, index_x)
    current = current + jnp.where(index_y == 0, through, 0.0)
    owner = own_ref[...]
    low = owner & (LANES - 1)
    picked = jnp.where(
        ((owner >> 7) & 1) == 1, lookup(current[:, LANES:], low), lookup(current[:, :LANES], low)
    )
    picked = jnp.where((owner >> 8) == die * 4 + index_x, picked, 0.0)
    send_ref[pl.ds(0, 64, stride=2), :] = jnp.where(half, picked, 0.0)
    send_ref[pl.ds(1, 64, stride=2), :] = jnp.where(half, pltpu.roll(picked, 64, 1), 0.0)
    for k in range(states_ref.shape[1]):
        fade = decay_ref[0, k]
        for t in range(8):
            at = slice(t * LANES, (t + 1) * LANES)
            old = fade * state_ref[0, k : k + 1, at] + volts_ref[t : t + 1, :]
            states_ref[0, k : k + 1, at] = fade * old + volts[t : t + 1, :]
    owner = jnp.concatenate([owner_ref[...], owner_ref[...]], 1)
    owner = jnp.broadcast_to(owner, (8, LANES))
    mine_ref[...] = fetch(cur_tab, owner >> 7, owner & (LANES - 1))[0:1]


def source_kernel(e_in, mine_ref, line_ref, cell_ref, e_ref, y_out, z_out):
    del e_in
    add_sources(e_ref, 2, cell_ref, mine_ref[...] * line_ref[0:1, :], cell_ref.shape[0])
    electric_edges(e_ref, y_out, z_out)


def body(
    e_field, h_field, material, decay_table, curl_table, residues, pole_decay,
    pole_states, direct, port_cell, port_owner,
):
    field, (nx, ny, nz) = e_field.shape, material.shape
    slots = port_cell.shape[0]
    devices = lax.axis_size(ALL)
    rows, ports = residues.shape[2:]
    where = jnp.stack([lax.axis_index(name) for name in ALL]).astype(I32)
    y_edge, z_edge = ((2 * nx, nz), F32), ((ny, LANES), F32)
    table = pltpu.VMEM((8, LANES), F32)
    cells = port_cell.reshape(1, slots)
    owners = port_owner.reshape(1, slots)

    def edges_back(y, z):
        return shifted(y, ("gx", "gy"), -1), shifted(z, "gz", -1)

    def edges_on(y, z):
        return shifted(y, ("gx", "gy"), 1), shifted(z, "gz", 1)

    def magnetic(electric, old, y, z):
        return call(
            h_kernel, ((field, F32), y_edge, z_edge), (VMEM,) * 7, (table,)
        )(electric, old, material, decay_table, curl_table, y, z)

    send, y, z = call(
        sample_kernel, (((devices, LANES), F32), y_edge, z_edge), (VMEM, SMEM, VMEM)
    )(e_field, port_cell, owners)
    y, z = edges_back(y, z)
    recv = lax.all_to_all(send, ALL, 0, 0, tiled=True)
    sums, damped, base = call(
        residue_kernel,
        (((rows, ports), F32), ((rows, ports), F32), ((8, rows), F32)),
        (VMEM, SMEM, VMEM),
        (pltpu.VMEM((8, ports), F32), pltpu.VMEM((2, rows, LANES), F32)),
    )(residues, pole_decay, pole_states)
    (line,) = call(slot_kernel, (((8, LANES), F32),), (VMEM, VMEM, SMEM, VMEM), (table,))(
        material, curl_table, port_cell, cells
    )
    h_one, y, z = magnetic(e_field, h_field, y, z)
    y, z = edges_on(y, z)
    own, at, volts, current = call(
        first_kernel,
        (((64, LANES), I32), ((2, 8, LANES), I32), ((8, LANES), F32), ((1, rows), F32)),
        (VMEM, VMEM, VMEM, VMEM, SMEM),
        (pltpu.VMEM((64, LANES), F32),),
    )(recv, sums, base, direct, where)
    e_one, got = call(
        e_kernel, ((field, F32), ((1, LANES), F32)), (VMEM,) * 7 + (SMEM,), (table,)
    )(e_field, h_one, material, decay_table, curl_table, y, z, port_cell)
    (send,) = call(pack_kernel, (((4 * devices, LANES), F32),), (VMEM,) * 3)(got, line, current)
    recv = lax.all_to_all(send, ALL, 0, 0, tiled=True)
    states, send, mine = call(
        second_kernel,
        ((pole_states.shape, F32), ((devices, LANES), F32), ((1, LANES), F32)),
        (VMEM,) * 8 + (SMEM, VMEM, VMEM, SMEM),
        (
            pltpu.VMEM((64, LANES), F32),
            pltpu.VMEM((64, LANES), F32),
            pltpu.VMEM((64, LANES), F32),
            pltpu.VMEM((72, LANES), F32),
            pltpu.VMEM((8, LANES), F32),
        ),
    )(recv, own, at, volts, sums, damped, base, direct, pole_decay, pole_states, owners, where)
    e_one, y, z = call(
        source_kernel, ((field, F32), y_edge, z_edge), (VMEM, VMEM, VMEM, SMEM), aliases={0: 0}
    )(e_one, mine, line, port_cell)
    y, z = edges_back(y, z)
    recv = lax.all_to_all(send, ALL, 0, 0, tiled=True)
    h_two, y, z = magnetic(e_one, h_one, y, z)
    y, z = edges_on(y, z)
    e_out, h_out, ez = call(
        e_last_kernel,
        ((field, F32), (field, F32), (field[1:], F32)),
        (VMEM,) * 7,
        (
            table,
            pltpu.VMEM((2,) + field[1:], F32),
            pltpu.SemaphoreType.DMA((2,)),
            pltpu.SemaphoreType.DMA,
        ),
        specs_out=(ANY, ANY, VMEM),
    )(e_one, h_two, material, decay_table, curl_table, y, z)
    (e_out,) = call(
        finish_kernel,
        ((field, F32),),
        (ANY, VMEM, VMEM, VMEM, SMEM),
        (pltpu.VMEM((1,) + field[1:], F32), pltpu.SemaphoreType.DMA),
        aliases={0: 0},
        specs_out=(ANY,),
    )(e_out, ez, recv, line[0:1], port_cell)
    return e_out, h_out, states


def solution(mesh):
    return jax.shard_map(
        body,
        mesh=mesh,
        in_specs=(
            P(None, None, ("gx", "gy"), "gz"),
            P(None, None, ("gx", "gy"), "gz"),
            P(None, ("gx", "gy"), "gz"),
            P(),
            P(),
            P("gz", "gy", "gx", None),
            P("gz", "gy"),
            P("gz", "gy", None),
            P("gz", "gx"),
            P(("gx", "gy", "gz")),
            P(("gx", "gy", "gz")),
        ),
        out_specs=(
            P(None, None, ("gx", "gy"), "gz"),
            P(None, None, ("gx", "gy"), "gz"),
            P("gz", "gy", None),
        ),
        check_vma=False,
    )
```

time: 503 us -> 135 us (0.27)
  the two profiles are of different devices: /device:TPU:7 before, /device:TPU:64 now
where the time goes in v1:
time: 135 us
  Pallas kernels  44.6 us (33%)
  starting transfers between devices  42.1 us (31%)
  local copies, waits for them, and re-layouts  23 us (17%)
  blocking collectives  17.8 us (13%)
  waiting for transfers between devices  6.04 us (4%)
    ppermute x8, starting transfers between devices, shifted(): lax.ppermute(value, axis, [(source, source + steps) for source in range(i...  24.7 us
    unnamed x46, local copies, waits for them, and re-layouts  23 us
    all_to_all x1, blocking collectives, body(): recv = lax.all_to_all(send, ALL, 0, 0, tiled=True)  17.8 us
    all_to_all x2, starting transfers between devices, body(): recv = lax.all_to_all(send, ALL, 0, 0, tiled=True)  17.4 us
    pallas_call x2, Pallas kernels, magnetic(): call(h_kernel, ((field, F32), y_edge, z_edge), (VMEM,) * 7, (table,))  13.9 us
    pallas_call x1, Pallas kernels, body(): call(e_kernel, ((field, F32), ((1, LANES), F32)), (VMEM,) * 7 + (SMEM,),...  6.59 us
    ppermute x8, waiting for transfers between devices, shifted(): lax.ppermute(value, axis, [(source, source + steps) for source in range(i...  6.03 us
    pallas_call x1, Pallas kernels, body(): call(e_last_kernel, ((field, F32), (field, F32), (field[1:], F32)), (VMEM...  5.87 us
  transfers between devices with their start and end apart: 10, of which 1 were waited for; matrix products, arithmetic and copies ran while one was open for 0% of the time, Pallas kernels for 18%

profile of v1, /device:TPU:64, one launch (start us, length us, event | category | flops | bytes accessed | tf_op | source)
XLA Modules:
  0.0 134.7 jit_solution(6742707933511342680)
XLA Ops:
  0.7 2.3 %copy-done = f32[3,24,64,256]{3,2,1,0:T(8,128)S(1)} copy-done((f32[3,24,64,256]{3,2,1,0:T(8,128)S(1)}, f32[3,24,64,256]{3,2,1,0:T(8,128)}, u32[]{:S(2)}) %copy-start) | copy-done | bytes 4718616
  4.3 4.0 %shard_map.130 = (f32[128,128]{1,0:T(8,128)}, f32[48,256]{1,0:T(8,128)S(1)}, f32[64,128]{1,0:T(8,128)S(1)}) custom-call(f32[3,24,64,256]{3,2,1,0:T(8,128)S(1)} %copy-done, s32[64]{0:T(128)S(1)} %copy-done.16, s32[1,64]{1,0:T(1,128)S(1)} %bitcast.20), custom_call_target="tpu_custom_call" | custom-call | tf_op jit(solution)/shard_map/pallas_call | solution.py:487
  9.5 3.8 %collective-permute-start.1 = (f32[64,128]{1,0:T(8,128)S(1)}, f32[64,128]{1,0:T(8,128)S(1)}, u32[]{:S(2)}, u32[]{:S(2)}) collective-permute-start(f32[64,128]{1,0:T(8,128)S(1)} %get-tuple-element.31), channel_id=1, source_target_pairs={{1,0},{2,1},{3,2},{4,3},{5,4},{6,5},{7,6},{9,8},{10,9},{11,10},{12... | collective-permute-start | bytes 98312 | tf_op jit(solution)/shard_map/ppermute | solution.py:32
  13.3 9.9 %all-to-all-start = ((f32[128,1,128]{2,1,0:T(1,128)}), f32[128,1,128]{2,1,0:T(1,128)S(1)}, u32[]{:S(2)}, u32[]{:S(2)}) async-start(f32[128,1,128]{2,1,0:T(1,128)} %bitcast.3), calls=%async_computation | async-start | bytes 131072 | tf_op jit(solution)/shard_map/all_to_all | solution.py:491
  23.4 2.3 %copy-done.1 = f32[3,24,64,256]{3,2,1,0:T(8,128)S(1)} copy-done((f32[3,24,64,256]{3,2,1,0:T(8,128)S(1)}, f32[3,24,64,256]{3,2,1,0:T(8,128)}, u32[]{:S(2)}) %copy-start.1) | copy-done | bytes 4718616
  25.7 2.3 %copy-done.10 = f32[3,24,64,256]{3,2,1,0:T(8,128)S(1)} copy-done((f32[3,24,64,256]{3,2,1,0:T(8,128)S(1)}, f32[3,24,64,256]{3,2,1,0:T(8,128)}, u32[]{:S(2)}) %copy-start.10) | copy-done | bytes 4718616
  28.0 6.9 %shard_map.131 = (f32[3,24,64,256]{3,2,1,0:T(8,128)S(1)}, f32[48,256]{1,0:T(8,128)S(1)}, f32[64,128]{1,0:T(8,128)S(1)}) custom-call(f32[3,24,64,256]{3,2,1,0:T(8,128)S(1)} %copy-done.1, f32[3,24,64,256]{3,2,1,0:T(8,128)S(1)} %copy-done.10, s32[24,64,256]{2,1,0:T(8,128)S(1)} %copy-done.6, f32[2,16]{1,0:T(2,128)S(1)} %copy-done.18, f32[2,16]{1,0:T(2,128)S(1)} %copy-done.15, ...), custom_call_target="tpu_custom_call" | custom-call | tf_op jit(solution)/shard_map/pallas_call | solution.py:483
  37.2 3.5 %collective-permute-start.3 = (f32[64,128]{1,0:T(8,128)S(1)}, f32[64,128]{1,0:T(8,128)S(1)}, u32[]{:S(2)}, u32[]{:S(2)}) collective-permute-start(f32[64,128]{1,0:T(8,128)S(1)} %get-tuple-element.34), channel_id=1, source_target_pairs={{0,1},{1,2},{2,3},{3,4},{4,5},{5,6},{6,7},{8,9},{9,10},{10,11},{11... | collective-permute-start | bytes 98312 | tf_op jit(solution)/shard_map/ppermute | solution.py:32
  40.7 3.4 %collective-permute-start.2 = (f32[48,256]{1,0:T(8,128)S(1)}, f32[48,256]{1,0:T(8,128)S(1)}, u32[]{:S(2)}, u32[]{:S(2)}) collective-permute-start(f32[48,256]{1,0:T(8,128)S(1)} %get-tuple-element.33), channel_id=1, source_target_pairs={{0,8},{8,16},{16,24},{24,32},{32,40},{40,48},{48,56},{56,64},{64,7... | collective-permute-start | bytes 147464 | tf_op jit(solution)/shard_map/ppermute | solution.py:32
  50.3 2.3 %copy-done.2 = f32[3,24,64,256]{3,2,1,0:T(8,128)S(1)} copy-done((f32[3,24,64,256]{3,2,1,0:T(8,128)S(1)}, f32[3,24,64,256]{3,2,1,0:T(8,128)}, u32[]{:S(2)}) %copy-start.2) | copy-done | bytes 4718616
  52.6 2.3 %copy-done.8 = f32[3,24,64,256]{3,2,1,0:T(8,128)S(1)} copy-done((f32[3,24,64,256]{3,2,1,0:T(8,128)S(1)}, f32[3,24,64,256]{3,2,1,0:T(8,128)}, u32[]{:S(2)}) %copy-start.8) | copy-done | bytes 4718616
  55.0 6.6 %shard_map.132 = (f32[3,24,64,256]{3,2,1,0:T(8,128)S(1)}, f32[1,128]{1,0:T(1,128)S(1)}) custom-call(f32[3,24,64,256]{3,2,1,0:T(8,128)S(1)} %copy-done.2, f32[3,24,64,256]{3,2,1,0:T(8,128)S(1)} %copy-done.8, s32[24,64,256]{2,1,0:T(8,128)S(1)} %copy-done.6, f32[2,16]{1,0:T(2,128)S(1)} %copy-done.18, f32[2,16]{1,0:T(2,128)S(1)} %copy-done.15, ...), custom_call_target="tpu_custom_call" | custom-call | tf_op jit(solution)/shard_map/pallas_call | solution.py:509
  61.7 17.8 %all_to_all.33 = f32[128,4,128]{2,1,0:T(4,128)S(1)} all-to-all(f32[128,4,128]{2,1,0:T(4,128)S(1)} %bitcast.16), channel_id=1, replica_groups=mesh['gx'=4,'gy'=4,'gz'=8] {'gx','gy','gz'}, dimensions={0} | all-to-all | bytes 524288 | tf_op jit(solution)/shard_map/all_to_all | solution.py:513
  81.4 4.0 %shard_map.138 = (f32[3,24,64,256]{3,2,1,0:T(8,128)S(1)}, f32[48,256]{1,0:T(8,128)S(1)}, f32[64,128]{1,0:T(8,128)S(1)}) custom-call(f32[3,24,64,256]{3,2,1,0:T(8,128)S(1)} %get-tuple-element.35.e_in, f32[1,128]{1,0:T(1,128)S(1)} %get-tuple-element.45.mine_ref, f32[8,128]{1,0:T(8,128)S(1)} %shard_map.133.line_ref, ...), custom_call_target="tpu_custom_call", output_to_operand_aliasing={{0}: (0, {})} | custom-call | tf_op jit(solution)/shard_map/pallas_call | solution.py:526
  88.9 4.6 %collective-permute-start.5 = (f32[64,128]{1,0:T(8,128)S(1)}, f32[64,128]{1,0:T(8,128)S(1)}, u32[]{:S(2)}, u32[]{:S(2)}) collective-permute-start(f32[64,128]{1,0:T(8,128)S(1)} %get-tuple-element.48), channel_id=1, source_target_pairs={{1,0},{2,1},{3,2},{4,3},{5,4},{6,5},{7,6},{9,8},{10,9},{11,10},{12... | collective-permute-start | bytes 98312 | tf_op jit(solution)/shard_map/ppermute | solution.py:32
  93.5 7.5 %all-to-all-start.2 = ((f32[128,1,128]{2,1,0:T(1,128)}), f32[128,1,128]{2,1,0:T(1,128)S(1)}, u32[]{:S(2)}, u32[]{:S(2)}) async-start(f32[128,1,128]{2,1,0:T(1,128)} %bitcast.11), calls=%async_computation.2 | async-start | bytes 131072 | tf_op jit(solution)/shard_map/all_to_all | solution.py:530
  101.1 2.3 %copy-done.4 = f32[3,24,64,256]{3,2,1,0:T(8,128)S(1)} copy-done((f32[3,24,64,256]{3,2,1,0:T(8,128)S(1)}, f32[3,24,64,256]{3,2,1,0:T(8,128)}, u32[]{:S(2)}) %copy-start.4) | copy-done | bytes 4718616
  103.4 2.3 %copy-done.9 = f32[3,24,64,256]{3,2,1,0:T(8,128)S(1)} copy-done((f32[3,24,64,256]{3,2,1,0:T(8,128)S(1)}, f32[3,24,64,256]{3,2,1,0:T(8,128)}, u32[]{:S(2)}) %copy-start.9) | copy-done | bytes 4718616
  105.7 7.0 %shard_map.139 = (f32[3,24,64,256]{3,2,1,0:T(8,128)S(1)}, f32[48,256]{1,0:T(8,128)S(1)}, f32[64,128]{1,0:T(8,128)S(1)}) custom-call(f32[3,24,64,256]{3,2,1,0:T(8,128)S(1)} %copy-done.4, f32[3,24,64,256]{3,2,1,0:T(8,128)S(1)} %copy-done.9, s32[24,64,256]{2,1,0:T(8,128)S(1)} %copy-done.6, f32[2,16]{1,0:T(2,128)S(1)} %copy-done.18, f32[2,16]{1,0:T(2,128)S(1)} %copy-done.15, ...), custom_call_target="tpu_custom_call" | custom-call | tf_op jit(solution)/shard_map/pallas_call | solution.py:483
  112.7 3.4 %collective-permute-start.6 = (f32[48,256]{1,0:T(8,128)S(1)}, f32[48,256]{1,0:T(8,128)S(1)}, u32[]{:S(2)}, u32[]{:S(2)}) collective-permute-start(f32[48,256]{1,0:T(8,128)S(1)} %get-tuple-element.50), channel_id=1, source_target_pairs={{0,8},{8,16},{16,24},{24,32},{32,40},{40,48},{48,56},{56,64},{64,7... | collective-permute-start | bytes 147464 | tf_op jit(solution)/shard_map/ppermute | solution.py:32
  116.2 3.4 %collective-permute-start.7 = (f32[64,128]{1,0:T(8,128)S(1)}, f32[64,128]{1,0:T(8,128)S(1)}, u32[]{:S(2)}, u32[]{:S(2)}) collective-permute-start(f32[64,128]{1,0:T(8,128)S(1)} %get-tuple-element.51), channel_id=1, source_target_pairs={{0,1},{1,2},{2,3},{3,4},{4,5},{5,6},{6,7},{8,9},{9,10},{10,11},{11... | collective-permute-start | bytes 98312 | tf_op jit(solution)/shard_map/ppermute | solution.py:32
  119.6 6.0 %collective-permute-done.7.zl_ref = f32[64,128]{1,0:T(8,128)S(1)} collective-permute-done((f32[64,128]{1,0:T(8,128)S(1)}, f32[64,128]{1,0:T(8,128)S(1)}, u32[]{:S(2)}, u32[]{:S(2)}) %collective-permute-start.7) | collective-permute-done | bytes 32800 | tf_op jit(solution)/shard_map/ppermute | solution.py:32
  125.6 5.9 %shard_map.140 = (f32[3,24,64,256]{3,2,1,0:T(8,128)}, f32[3,24,64,256]{3,2,1,0:T(8,128)}, f32[24,64,256]{2,1,0:T(8,128)S(1)}) custom-call(f32[3,24,64,256]{3,2,1,0:T(8,128)S(1)} %copy-done.5, f32[3,24,64,256]{3,2,1,0:T(8,128)S(1)} %get-tuple-element.49.h_ref, s32[24,64,256]{2,1,0:T(8,128)S(1)} %copy-done.6, f32[2,16]{1,0:T(2,128)S(1)} %copy-done.18, ...), custom_call_target="tpu_custom_call" | custom-call | tf_op jit(solution)/shard_map/pallas_call | solution.py:533
  131.5 3.2 %shard_map.141 = f32[3,24,64,256]{3,2,1,0:T(8,128)} custom-call(f32[3,24,64,256]{3,2,1,0:T(8,128)} %get-tuple-element.52.e_in, f32[24,64,256]{2,1,0:T(8,128)S(1)} %get-tuple-element.53.ez_ref, f32[128,128]{1,0:T(8,128)S(1)} %bitcast.17, f32[1,128]{1,0:T(1,128)S(1)} %slice.3.curl_ref, s32[64]{0:T(128)S(1)} %copy-done.17), custom_call_target="tpu_custom_call", output_to_operand_aliasing={{}: (0, {})} | custom-call | tf_op jit(solution)/shard_map/pallas_call | solution.py:545
  (57 shorter events, 16.4 us)
Async XLA Ops:
  0.6 22.7 %copy-start.15 = (f32[2,16]{1,0:T(2,128)S(1)}, f32[2,16]{1,0:T(2,128)}, u32[]{:S(2)}) copy-start(f32[2,16]{1,0:T(2,128)} %curl_ref.9) | copy-start | bytes 388
  0.6 2.3 %copy-start = (f32[3,24,64,256]{3,2,1,0:T(8,128)S(1)}, f32[3,24,64,256]{3,2,1,0:T(8,128)}, u32[]{:S(2)}) copy-start(f32[3,24,64,256]{3,2,1,0:T(8,128)} %e_ref.5) | copy-start | bytes 14155780
  4.3 19.0 %copy-start.6 = (s32[24,64,256]{2,1,0:T(8,128)S(1)}, s32[24,64,256]{2,1,0:T(8,128)}, u32[]{:S(2)}) copy-start(s32[24,64,256]{2,1,0:T(8,128)} %mat_ref.9) | copy-start | bytes 4718596
  4.3 19.0 %copy-start.18 = (f32[2,16]{1,0:T(2,128)S(1)}, f32[2,16]{1,0:T(2,128)}, u32[]{:S(2)}) copy-start(f32[2,16]{1,0:T(2,128)} %decay_ref.11) | copy-start | bytes 388
  8.3 15.0 %collective-permute-start = (f32[48,256]{1,0:T(8,128)S(1)}, f32[48,256]{1,0:T(8,128)S(1)}, u32[]{:S(2)}, u32[]{:S(2)}) collective-permute-start(f32[48,256]{1,0:T(8,128)S(1)} %get-tuple-element.30), channel_id=1, source_target_pairs={{8,0},{16,8},{24,16},{32,24},{40,32},{48,40},{56,48},{64,56},{72,6... | collective-permute-start | bytes 147464 | tf_op jit(solution)/shard_map/ppermute | solution.py:32
  9.5 13.7 %collective-permute-start.1 = (f32[64,128]{1,0:T(8,128)S(1)}, f32[64,128]{1,0:T(8,128)S(1)}, u32[]{:S(2)}, u32[]{:S(2)}) collective-permute-start(f32[64,128]{1,0:T(8,128)S(1)} %get-tuple-element.31), channel_id=1, source_target_pairs={{1,0},{2,1},{3,2},{4,3},{5,4},{6,5},{7,6},{9,8},{10,9},{11,10},{12... | collective-permute-start | bytes 98312 | tf_op jit(solution)/shard_map/ppermute | solution.py:32
  13.3 35.4 %all-to-all-start = ((f32[128,1,128]{2,1,0:T(1,128)}), f32[128,1,128]{2,1,0:T(1,128)S(1)}, u32[]{:S(2)}, u32[]{:S(2)}) async-start(f32[128,1,128]{2,1,0:T(1,128)} %bitcast.3), calls=%async_computation | async-start | bytes 131072 | tf_op jit(solution)/shard_map/all_to_all | solution.py:491
  23.3 20.9 %copy-start.17 = (s32[64]{0:T(128)S(1)}, s32[64]{0:T(128)}, u32[]{:S(2)}) copy-start(s32[64]{0:T(128)} %cell_ref.9) | copy-start | bytes 772
  23.3 22.4 %copy-start.22 = (f32[1,4]{1,0:T(1,128)S(1)}, f32[1,4]{1,0:T(1,128)}, u32[]{:S(2)}) copy-start(f32[1,4]{1,0:T(1,128)} %decay_ref.9) | copy-start | bytes 52
  23.3 2.3 %copy-start.1 = (f32[3,24,64,256]{3,2,1,0:T(8,128)S(1)}, f32[3,24,64,256]{3,2,1,0:T(8,128)}, u32[]{:S(2)}) copy-start(f32[3,24,64,256]{3,2,1,0:T(8,128)} %e_ref.5) | copy-start | bytes 14155780
  28.0 17.7 %copy-start.11 = (f32[1,4,256,1024]{3,2,1,0:T(8,128)S(1)}, f32[1,4,256,1024]{3,2,1,0:T(8,128)}, u32[]{:S(2)}) copy-start(f32[1,4,256,1024]{3,2,1,0:T(8,128)} %res_ref.1) | copy-start | bytes 12582916
  28.0 17.7 %copy-start.14 = (f32[1,4,1024]{2,1,0:T(4,128)S(1)}, f32[1,4,1024]{2,1,0:T(4,128)}, u32[]{:S(2)}) copy-start(f32[1,4,1024]{2,1,0:T(4,128)} %state_ref.3) | copy-start | bytes 49156
  37.2 11.6 %copy-start.19 = (f32[1,256]{1,0:T(1,128)S(1)}, f32[1,256]{1,0:T(1,128)}, u32[]{:S(2)}) copy-start(f32[1,256]{1,0:T(1,128)} %direct_ref.3) | copy-start | bytes 3076
  37.2 13.1 %collective-permute-start.3 = (f32[64,128]{1,0:T(8,128)S(1)}, f32[64,128]{1,0:T(8,128)S(1)}, u32[]{:S(2)}, u32[]{:S(2)}) collective-permute-start(f32[64,128]{1,0:T(8,128)S(1)} %get-tuple-element.34), channel_id=1, source_target_pairs={{0,1},{1,2},{2,3},{3,4},{4,5},{5,6},{6,7},{8,9},{9,10},{10,11},{11... | collective-permute-start | bytes 98312 | tf_op jit(solution)/shard_map/ppermute | solution.py:32
  40.7 9.6 %collective-permute-start.2 = (f32[48,256]{1,0:T(8,128)S(1)}, f32[48,256]{1,0:T(8,128)S(1)}, u32[]{:S(2)}, u32[]{:S(2)}) collective-permute-start(f32[48,256]{1,0:T(8,128)S(1)} %get-tuple-element.33), channel_id=1, source_target_pairs={{0,8},{8,16},{16,24},{24,32},{32,40},{40,48},{48,56},{56,64},{64,7... | collective-permute-start | bytes 147464 | tf_op jit(solution)/shard_map/ppermute | solution.py:32
  50.3 2.3 %copy-start.2 = (f32[3,24,64,256]{3,2,1,0:T(8,128)S(1)}, f32[3,24,64,256]{3,2,1,0:T(8,128)}, u32[]{:S(2)}) copy-start(f32[3,24,64,256]{3,2,1,0:T(8,128)} %e_ref.5) | copy-start | bytes 14155780
  55.0 24.6 %copy-start.13 = (f32[256,1024]{1,0:T(8,128)S(1)}, f32[256,1024]{1,0:T(8,128)}, u32[]{:S(2)}) copy-start(f32[256,1024]{1,0:T(8,128)} %copy-done.12) | copy-start | bytes 3145732
  55.0 24.6 %copy-start.21 = (s32[64]{0:T(128)S(1)}, s32[64]{0:T(128)}, u32[]{:S(2)}) copy-start(s32[64]{0:T(128)} %param.21) | copy-start | bytes 772
  87.6 13.4 %collective-permute-start.4 = (f32[48,256]{1,0:T(8,128)S(1)}, f32[48,256]{1,0:T(8,128)S(1)}, u32[]{:S(2)}, u32[]{:S(2)}) collective-permute-start(f32[48,256]{1,0:T(8,128)S(1)} %get-tuple-element.47), channel_id=1, source_target_pairs={{8,0},{16,8},{24,16},{32,24},{40,32},{48,40},{56,48},{64,56},{72,6... | collective-permute-start | bytes 147464 | tf_op jit(solution)/shard_map/ppermute | solution.py:32
  88.9 12.1 %collective-permute-start.5 = (f32[64,128]{1,0:T(8,128)S(1)}, f32[64,128]{1,0:T(8,128)S(1)}, u32[]{:S(2)}, u32[]{:S(2)}) collective-permute-start(f32[64,128]{1,0:T(8,128)S(1)} %get-tuple-element.48), channel_id=1, source_target_pairs={{1,0},{2,1},{3,2},{4,3},{5,4},{6,5},{7,6},{9,8},{10,9},{11,10},{12... | collective-permute-start | bytes 98312 | tf_op jit(solution)/shard_map/ppermute | solution.py:32
  93.5 37.9 %all-to-all-start.2 = ((f32[128,1,128]{2,1,0:T(1,128)}), f32[128,1,128]{2,1,0:T(1,128)S(1)}, u32[]{:S(2)}, u32[]{:S(2)}) async-start(f32[128,1,128]{2,1,0:T(1,128)} %bitcast.11), calls=%async_computation.2 | async-start | bytes 131072 | tf_op jit(solution)/shard_map/all_to_all | solution.py:530
  105.7 19.9 %copy-start.5 = (f32[3,24,64,256]{3,2,1,0:T(8,128)S(1)}, f32[3,24,64,256]{3,2,1,0:T(8,128)}, u32[]{:S(2)}) copy-start(f32[3,24,64,256]{3,2,1,0:T(8,128)} %copy-done.3) | copy-start | bytes 14155780
  112.7 12.9 %collective-permute-start.6 = (f32[48,256]{1,0:T(8,128)S(1)}, f32[48,256]{1,0:T(8,128)S(1)}, u32[]{:S(2)}, u32[]{:S(2)}) collective-permute-start(f32[48,256]{1,0:T(8,128)S(1)} %get-tuple-element.50), channel_id=1, source_target_pairs={{0,8},{8,16},{16,24},{24,32},{32,40},{40,48},{48,56},{56,64},{64,7... | collective-permute-start | bytes 147464 | tf_op jit(solution)/shard_map/ppermute | solution.py:32
  116.2 9.4 %collective-permute-start.7 = (f32[64,128]{1,0:T(8,128)S(1)}, f32[64,128]{1,0:T(8,128)S(1)}, u32[]{:S(2)}, u32[]{:S(2)}) collective-permute-start(f32[64,128]{1,0:T(8,128)S(1)} %get-tuple-element.51), channel_id=1, source_target_pairs={{0,1},{1,2},{2,3},{3,4},{4,5},{5,6},{6,7},{8,9},{9,10},{10,11},{11... | collective-permute-start | bytes 98312 | tf_op jit(solution)/shard_map/ppermute | solution.py:32
  (9 other events, 16.0 us)

commit v2 on v1

--- a/solution.py
+++ b/solution.py
@@ -5,13 +5,15 @@
 from jax.experimental.pallas import tpu as pltpu
 from jax.sharding import PartitionSpec as P
 
+
 ALL = ("gx", "gy", "gz")
 F32 = jnp.float32
 I32 = jnp.int32
 LANES = 128
+UNROLL = 2
 VMEM = pl.BlockSpec(memory_space=pltpu.VMEM)
 SMEM = pl.BlockSpec(memory_space=pltpu.SMEM)
-ANY = pl.BlockSpec(memory_space=pl.ANY)
+HBM = pl.BlockSpec(memory_space=pltpu.HBM)
 
 
 def call(kernel, outs, ins, scratch=(), aliases=None, limit=16, specs_out=None):
@@ -26,6 +28,10 @@
     )
 
 
+def in_hbm(value):
+    return pltpu.with_memory_space_constraint(value, pltpu.HBM)
+
+
 def shifted(value, axis, steps):
     count = lax.axis_size(axis)
     initial, last = (max(0, -steps), min(count, count - steps))
@@ -49,6 +55,14 @@
 def table_lookup(row, index):
     half = index.shape[1] // 2
     return jnp.concatenate([lookup(row, index[:, :half]), lookup(row, index[:, half:])], 1)
+
+
+def tree_lookup(entries, bits):
+    for bit in bits:
+        entries = [
+            jnp.where(bit, odd, even) for even, odd in zip(entries[0::2], entries[1::2])
+        ]
+    return entries[0]
 
 
 def load_tables(scratch, decay_ref, curl_ref):
@@ -71,42 +85,95 @@
         moved = pltpu.roll(half, (slot - k) & (LANES - 1), 1)
         return jnp.where(lane == slot, moved, acc)
 
-    return lax.fori_loop(0, count, step, jnp.zeros((1, LANES), F32), unroll=8)
-
-
-def add_sources(field_ref, comp, cell_ref, values, count):
-    lane = lane_iota((1, 2 * LANES))
-    wide = jnp.broadcast_to(values, (8, LANES))
-
-    def step(slot, carry):
-        i, y, k = cell_of(cell_ref[slot])
-        splat = lookup(wide[0:1], jnp.full((8, LANES), slot, I32))[0:1]
-        both = jnp.concatenate([splat, splat], 1)
-        row = field_ref[comp, i, pl.ds(y, 1), :]
-        field_ref[comp, i, pl.ds(y, 1), :] = row - jnp.where(lane == k, both, 0.0)
-        return carry
-
-    lax.fori_loop(0, count, step, 0, unroll=4)
-
-
-def electric_edges(e_ref, y_out, z_out):
-    nx, ny = e_ref.shape[1], e_ref.shape[2]
+    return lax.fori_loop(0, count, step, jnp.zeros((1, LANES), F32), unroll=count)
+
+
+def split3(value):
+    high = value.astype(jnp.bfloat16)
+    rest = value - high.astype(F32)
+    middle = rest.astype(jnp.bfloat16)
+    return high, middle, (rest - middle.astype(F32)).astype(jnp.bfloat16)
+
+
+def add_sources(field_ref, lead, cell_ref, values, same_ref, mark_ref, work):
+    count = cell_ref.shape[0]
+    scaled = same_ref[...] * values[:, :count]
+    marks = mark_ref[...].astype(jnp.bfloat16)
+    total = None
+    for part in split3(scaled):
+        product = jnp.dot(part, marks, preferred_element_type=F32)
+        total = product if total is None else total + product
+    work[...] = total
+    for slot in range(count):
+        i, y, _ = cell_of(cell_ref[slot])
+        row = field_ref[lead + (i, pl.ds(y, 1))]
+        work[slot : slot + 1, :] = row - work[slot : slot + 1, :]
+    for slot in range(count):
+        i, y, _ = cell_of(cell_ref[slot])
+        field_ref[lead + (i, pl.ds(y, 1))] = work[slot : slot + 1, :]
+
+
+def electric_edges(nx, first_row, first_tile, y_out, z_out):
+    ny = z_out.shape[0]
     lane = lane_iota((ny, LANES))
 
     def step(i, acc):
-        y_out[pl.ds(i, 1), :] = e_ref[0, i, 0:1, :]
-        y_out[pl.ds(nx + i, 1), :] = e_ref[2, i, 0:1, :]
+        y_out[pl.ds(i, 1), :] = first_row(0, i)
+        y_out[pl.ds(nx + i, 1), :] = first_row(1, i)
         for c in range(2):
             j = c * nx + i
-            acc = jnp.where(lane == j, pltpu.roll(e_ref[c, i, :, 0:LANES], j, 1), acc)
+            acc = jnp.where(lane == j, pltpu.roll(first_tile(c, i), j, 1), acc)
         return acc
 
-    z_out[...] = lax.fori_loop(0, nx, step, jnp.zeros((ny, LANES), F32))
-
-
-def h_kernel(e_ref, h_ref, mat_ref, decay_ref, curl_ref, yh_ref, zh_ref, out_ref, yl_ref, zl_ref, tab):
+    z_out[...] = lax.fori_loop(0, nx, step, jnp.zeros((ny, LANES), F32), unroll=6)
+
+
+def factor_kernel(
+    mat_in, e_in, h_in, decay_ref, curl_ref, curl_sm,
+    magn_ref, elec_ref, e_ref, h_ref, tab, mat_ref, mat_sem, field_sem,
+):
+    parts = mat_sem.shape[0]
+    size = mat_ref.shape[0] // parts
+    copies = []
+    for p in range(parts):
+        at = slice(p * size, (p + 1) * size)
+        copies.append(pltpu.make_async_copy(mat_in.at[at], mat_ref.at[at], mat_sem.at[p]))
+    fields = [
+        pltpu.make_async_copy(e_in, e_ref, field_sem.at[0]),
+        pltpu.make_async_copy(h_in, h_ref, field_sem.at[1]),
+    ]
+    for copy in copies + fields:
+        copy.start()
     load_tables(tab, decay_ref, curl_ref)
-    nx, ny, nz = mat_ref.shape
+
+    def step(i, carry):
+        mat = mat_ref[i]
+        bits = [(mat & (1 << b)) != 0 for b in range(4)]
+        magn_ref[0, i] = table_lookup(tab[1:2, :], mat)
+        magn_ref[1, i] = table_lookup(tab[3:4, :], mat)
+        elec_ref[0, i] = table_lookup(tab[0:1, :], mat)
+        elec_ref[1, i] = tree_lookup([curl_sm[0, n] for n in range(16)], bits)
+        return carry
+
+    for p in range(parts):
+        copies[p].wait()
+        lax.fori_loop(p * size, (p + 1) * size, step, 0, unroll=UNROLL)
+    for copy in fields:
+        copy.wait()
+
+
+def h_kernel(e_ref, h_ref, magn_ref, yh_ref, zh_ref, out_ref, yl_ref, zl_ref):
+    def factors(i):
+        return magn_ref[0, i], magn_ref[1, i]
+
+    acc = jnp.zeros(zl_ref.shape, F32)
+    zl_ref[...] = h_update(
+        factors, e_ref, h_ref, yh_ref, zh_ref, out_ref, yl_ref, acc, 0, e_ref.shape[1]
+    )
+
+
+def h_update(factors, e_ref, h_ref, yh_ref, zh_ref, out_ref, yl_ref, acc, begin, end):
+    nx, ny, nz = e_ref.shape[1:]
     row = row_iota((ny, nz))
     lane = lane_iota((ny, LANES))
 
@@ -120,9 +187,7 @@
         return jnp.concatenate([moved[:, : nz - LANES], right], 1)
 
     def step(i, acc):
-        mat = mat_ref[i]
-        decay = table_lookup(tab[1:2, :], mat)
-        curl = table_lookup(tab[3:4, :], mat)
+        decay, curl = factors(i)
         ex, ey, ez = e_ref[0, i], e_ref[1, i], e_ref[2, i]
         after = jnp.minimum(i + 1, nx - 1)
         inside = i < nx - 1
@@ -146,11 +211,11 @@
             acc = jnp.where(lane == j, moved, acc)
         return acc
 
-    zl_ref[...] = lax.fori_loop(0, nx, step, jnp.zeros((ny, LANES), F32))
-
-
-def e_slab(i, e_ref, h_ref, mat_ref, yl_ref, zl_ref, tab):
-    nx, ny, nz = mat_ref.shape
+    return lax.fori_loop(begin, end, step, acc, unroll=UNROLL)
+
+
+def e_slab(i, e_ref, h_ref, elec_ref, yl_ref, zl_ref):
+    nx, ny, nz = e_ref.shape[1:]
     row = row_iota((ny, nz))
     lane = lane_iota((ny, LANES))
 
@@ -163,9 +228,7 @@
         left = jnp.where(lane == 0, halo, moved[:, :LANES])
         return jnp.concatenate([left, moved[:, LANES:]], 1)
 
-    mat = mat_ref[i]
-    decay = table_lookup(tab[0:1, :], mat)
-    curl = table_lookup(tab[2:3, :], mat)
+    decay, curl = elec_ref[0, i], elec_ref[1, i]
     hx, hy, hz = h_ref[0, i], h_ref[1, i], h_ref[2, i]
     before = jnp.maximum(i - 1, 0)
     inside = i > 0
@@ -181,27 +244,24 @@
     return ex, ey, ez
 
 
-def e_kernel(e_ref, h_ref, mat_ref, decay_ref, curl_ref, yl_ref, zl_ref, cell_ref, out_ref, got_ref, tab):
-    load_tables(tab, decay_ref, curl_ref)
-
+def e_kernel(e_ref, h_ref, elec_ref, yl_ref, zl_ref, cell_ref, out_ref, got_ref):
     def step(i, carry):
-        ex, ey, ez = e_slab(i, e_ref, h_ref, mat_ref, yl_ref, zl_ref, tab)
+        ex, ey, ez = e_slab(i, e_ref, h_ref, elec_ref, yl_ref, zl_ref)
         out_ref[0, i] = ex
         out_ref[1, i] = ey
         out_ref[2, i] = ez
         return carry
 
-    lax.fori_loop(0, mat_ref.shape[0], step, 0)
+    lax.fori_loop(0, e_ref.shape[1], step, 0, unroll=UNROLL)
     got_ref[...] = sample_rows(
         lambda i, y: out_ref[2, i, pl.ds(y, 1), :], cell_ref, cell_ref.shape[0]
     )
 
 
 def e_last_kernel(
-    e_ref, h_ref, mat_ref, decay_ref, curl_ref, yl_ref, zl_ref, e_out, h_out, ez_ref, tab, buf, sem, h_sem
+    e_ref, h_ref, elec_ref, yl_ref, zl_ref, e_out, h_out, ez_ref, buf, sem, h_sem
 ):
-    load_tables(tab, decay_ref, curl_ref)
-    nx = mat_ref.shape[0]
+    nx = e_ref.shape[1]
     h_copy = pltpu.make_async_copy(h_ref, h_out, h_sem)
     h_copy.start()
 
@@ -209,7 +269,7 @@
         return pltpu.make_async_copy(buf.at[c, i], e_out.at[c, i], sem.at[c])
 
     def step(i, carry):
-        ex, ey, ez = e_slab(i, e_ref, h_ref, mat_ref, yl_ref, zl_ref, tab)
+        ex, ey, ez = e_slab(i, e_ref, h_ref, elec_ref, yl_ref, zl_ref)
         buf[0, i] = ex
         buf[1, i] = ey
         ez_ref[i] = ez
@@ -217,33 +277,66 @@
         out_copy(i, 1).start()
         return carry
 
-    lax.fori_loop(0, nx, step, 0)
+    lax.fori_loop(0, nx, step, 0, unroll=UNROLL)
     for c in range(2):
         pltpu.make_async_copy(buf.at[c], e_out.at[c], sem.at[c]).wait()
     h_copy.wait()
 
 
-def finish_kernel(e_in, ez_ref, got_ref, curl_ref, cell_ref, e_out, work, sem):
-    del e_in
-    count = cell_ref.shape[0]
-    work[0] = ez_ref[...]
-    values = jnp.sum(got_ref[...], 0, keepdims=True) * curl_ref[...]
-    add_sources(work, 0, cell_ref, values, count)
-    copy = pltpu.make_async_copy(work.at[0], e_out.at[2], sem)
+def finish_kernel(
+    e_in, ez_in, got_ref, line_ref, cell_ref, same_ref, mark_ref, e_out, ez_ref, work, sem
+):
+    del e_in, ez_in
+    values = jnp.sum(got_ref[...], 0, keepdims=True) * line_ref[0:1, :]
+    add_sources(ez_ref, (), cell_ref, values, same_ref, mark_ref, work)
+    copy = pltpu.make_async_copy(ez_ref, e_out.at[2], sem)
     copy.start()
     copy.wait()
 
 
-def sample_kernel(e_ref, cell_ref, owner_ref, send_ref, y_out, z_out):
-    count = cell_ref.shape[0]
-    got = sample_rows(lambda i, y: e_ref[2, i, pl.ds(y, 1), :], cell_ref, count)
+def sample_kernel(
+    e_ref, cell_in, owner_in, send_ref, y_out, z_out,
+    cell_ref, owner_ref, slabs, rows, tiles, sems,
+):
+    count, nx = cell_in.shape[0], e_ref.shape[1]
+    cell_copy = pltpu.make_async_copy(cell_in, cell_ref, sems.at[0])
+    cell_copy.start()
+    owner_copy = pltpu.make_async_copy(owner_in, owner_ref, sems.at[1])
+    owner_copy.start()
+    y_copies = [
+        pltpu.make_async_copy(e_ref.at[2 * c, :, 0:8], rows.at[c], sems.at[4 + c])
+        for c in range(2)
+    ]
+    for copy in y_copies:
+        copy.start()
+    z_copy = pltpu.make_async_copy(e_ref.at[0:2, :, :, 0:LANES], tiles, sems.at[3])
+    z_copy.start()
+    cell_copy.wait()
+    for slot in range(count):
+        i, y, _ = cell_of(cell_ref[slot])
+        block = pl.ds(pl.multiple_of((y >> 3) << 3, 8), 8)
+        pltpu.make_async_copy(e_ref.at[2, i, block], slabs.at[slot], sems.at[2]).start()
+    owner_copy.wait()
+    pltpu.make_async_copy(slabs, slabs, sems.at[2]).wait()
+    lane = lane_iota((1, LANES))
+    got = jnp.zeros((1, LANES), F32)
+    for slot in range(count):
+        _, y, k = cell_of(cell_ref[slot])
+        row = slabs[slot, pl.ds(y & 7, 1), :]
+        half = jnp.where(k >= LANES, row[:, LANES:], row[:, :LANES])
+        got = jnp.where(lane == slot, pltpu.roll(half, (slot - k) & (LANES - 1), 1), got)
     owner = owner_ref[...].astype(F32)
     line = jnp.concatenate([got[:, :count], owner], 1)
     send_ref[...] = jnp.broadcast_to(line, send_ref.shape)
-    electric_edges(e_ref, y_out, z_out)
-
-
-def slot_kernel(mat_ref, curl_ref, cell_ref, cells_ref, line_ref, tab):
+    for copy in y_copies:
+        copy.wait()
+    z_copy.wait()
+    electric_edges(
+        nx, lambda c, i: rows[c, i, 0:1, :], lambda c, i: tiles[c, i], y_out, z_out
+    )
+
+
+def slot_kernel(mat_ref, curl_ref, cell_ref, cells_ref, line_ref, same_ref, mark_ref, tab):
     count = cell_ref.shape[0]
     tab[...] = jnp.zeros_like(tab)
     tab[0:1, 0:16] = curl_ref[0:1, :]
@@ -258,6 +351,12 @@
         twin = jnp.where(pltpu.roll(cells, r, 1) == cells, 1.0, twin)
     lane = lane_iota((1, LANES))
     line_ref[0:1, :] = jnp.where(lane < count, curl, 0.0)
+    wide = lane_iota((1, mark_ref.shape[1]))
+    grid_row = cells_ref[...] >> 8
+    for slot in range(count):
+        cell = cell_ref[slot]
+        same_ref[slot : slot + 1, :] = jnp.where(grid_row == (cell >> 8), 1.0, 0.0)
+        mark_ref[slot : slot + 1, :] = jnp.where(wide == (cell & 255), 1.0, 0.0)
     line_ref[1:2, :] = jnp.where(lane < count, cells.astype(F32), twin)
 
 
@@ -320,8 +419,8 @@
     )
 
 
-def first_kernel(recv_ref, sum_ref, base_ref, direct_ref, where_ref, own_ref, at_ref, volts_ref, cur_ref, tab):
-    index_x, index_y, die = where_ref[0], where_ref[1], where_ref[2]
+def first_kernel(recv_ref, sum_ref, base_ref, direct_ref, own_ref, at_ref, volts_ref, cur_ref, tab):
+    index_x, index_y, die = (lax.axis_index(name) for name in ALL)
     half = lane_iota((64, LANES)) < 64
     even = recv_ref[pl.ds(0, 64, stride=2), :]
     odd = recv_ref[pl.ds(1, 64, stride=2), :]
@@ -378,34 +477,26 @@
     lax.fori_loop(0, send_ref.shape[0] // 8, step, 0, unroll=8)
 
 
-def turn64(value, r):
-    lane = lane_iota(value.shape) & 63
+def turn64(value, r, lane):
     return jnp.where(
-        lane >= r, pltpu.roll(value, r, 1), pltpu.roll(value, (r + 64) & (LANES - 1), 1)
+        (lane & 63) >= r, pltpu.roll(value, r, 1), pltpu.roll(value, (r + 64) & (LANES - 1), 1)
     )
 
 
 def second_kernel(
-    recv_ref, own_ref, at_ref, volts_ref, sum_ref, damp_ref, base_ref, direct_ref,
-    decay_ref, state_ref, owner_ref, where_ref,
-    states_ref, send_ref, mine_ref,
-    cur_tab, ez_tab, curl_tab, shared, next_ref,
+    recv_ref, cur_tab, own_ref, at_ref, volts_ref, sum_ref, damp_ref, base_ref, direct_ref,
+    decay_ref, state_ref,
+    states_ref, send_ref,
+    ez_tab, curl_tab, cell_tab, shared, cur8, next_ref,
 ):
-    index_x, index_y, die = where_ref[0], where_ref[1], where_ref[2]
+    index_x, index_y, die = (lax.axis_index(name) for name in ALL)
     half = lane_iota((64, LANES)) < 64
-    for gx in range(4):
-        for h in range(2):
-            total = None
-            for gy in range(4):
-                part = recv_ref[pl.ds((gx * 4 + gy) * 32 + 1 + h, 8, stride=4), :]
-                total = part if total is None else total + part
-            cur_tab[pl.ds(gx * 2 + h, 8, stride=8), :] = total
     even = recv_ref[pl.ds(0, 64, stride=8), :]
     odd = recv_ref[pl.ds(4, 64, stride=8), :]
     ez_tab[...] = jnp.where(half, even, pltpu.roll(odd, 64, 1))
     curl_tab[...] = jnp.where(half, pltpu.roll(even, 64, 1), odd)
     rows, lanes = at_ref[0], at_ref[1]
-    shared[0:8, :] = cur_tab[pl.ds(pl.multiple_of(die * 8, 8), 8), :]
+    cur8[...] = cur_tab[pl.ds(pl.multiple_of(die * 8, 8), 8), :]
 
     even = recv_ref[pl.ds(3, 64, stride=8), :]
     odd = recv_ref[pl.ds(7, 64, stride=8), :]
@@ -413,23 +504,29 @@
 
     @pl.when(jnp.max(flags) > 0.5)
     def _():
-        cells = jnp.where(half, even, pltpu.roll(odd, 64, 1))
-        owner = own_ref[...]
-        high, low = owner >> 7, owner & (LANES - 1)
-
-        def pick(r, acc):
-            return jnp.where(high == r, lookup(cur_tab[pl.ds(r, 1), :], low), acc)
-
-        slots = lax.fori_loop(0, 64, pick, jnp.zeros((64, LANES), F32))
-
-        def gather(r, acc):
-            same = turn64(cells, r) == cells
-            return acc + jnp.where(same, turn64(slots, r), 0.0)
-
-        shared[8:72, :] = lax.fori_loop(1, 64, gather, slots)
-        shared[0:8, :] = fetch(shared.at[8:72], rows, lanes)
-
-    volts = fetch(ez_tab, rows, lanes) - fetch(curl_tab, rows, lanes) * shared[0:8, :]
+        cell_tab[...] = jnp.where(half, even, pltpu.roll(odd, 64, 1))
+        shared[...] = jnp.zeros_like(shared)
+        number = row_iota((64, LANES)).astype(F32)
+        line = lane_iota((1, LANES))
+
+        def one_row(left):
+            at = jnp.max(left).astype(I32) - 1
+            cells = cell_tab[pl.ds(at, 1), :]
+            owner = jnp.broadcast_to(own_ref[pl.ds(at, 1), :], (8, LANES))
+            slots = fetch(cur_tab, owner >> 7, owner & (LANES - 1))[0:1]
+            total = jnp.zeros((1, LANES), F32)
+            for r in range(1, 64):
+                same = turn64(cells, r, line) == cells
+                total = total + jnp.where(same, turn64(slots, r, line), 0.0)
+            shared[pl.ds(at, 1), :] = total
+            return jnp.where(number == (at.astype(F32)), 0.0, left)
+
+        marked = jnp.max(flags, 1, keepdims=True) > 0.5
+        left = jnp.where(jnp.broadcast_to(marked, (64, LANES)), number + 1.0, 0.0)
+        lax.while_loop(lambda left: jnp.max(left) > 0.5, one_row, left)
+        cur8[...] = cur8[...] + fetch(shared, rows, lanes)
+
+    volts = fetch(ez_tab, rows, lanes) - fetch(curl_tab, rows, lanes) * cur8[...]
     next_ref[...] = volts
     current = across(apply(sum_ref, volts) + apply(damp_ref, volts_ref[...])) + base_ref[1:2, :]
     through = direct_ref[...] * own_ports(next_ref, index_x)
@@ -448,15 +545,30 @@
             at = slice(t * LANES, (t + 1) * LANES)
             old = fade * state_ref[0, k : k + 1, at] + volts_ref[t : t + 1, :]
             states_ref[0, k : k + 1, at] = fade * old + volts[t : t + 1, :]
+
+
+def source_kernel(
+    e_in, recv_ref, owner_ref, line_ref, cell_ref, same_ref, mark_ref, e_ref, y_out, z_out, cur_tab, work
+):
+    del e_in
+    for gx in range(4):
+        for h in range(2):
+            total = None
+            for gy in range(4):
+                part = recv_ref[pl.ds((gx * 4 + gy) * 32 + 1 + h, 8, stride=4), :]
+                total = part if total is None else total + part
+            cur_tab[pl.ds(gx * 2 + h, 8, stride=8), :] = total
     owner = jnp.concatenate([owner_ref[...], owner_ref[...]], 1)
     owner = jnp.broadcast_to(owner, (8, LANES))
-    mine_ref[...] = fetch(cur_tab, owner >> 7, owner & (LANES - 1))[0:1]
-
-
-def source_kernel(e_in, mine_ref, line_ref, cell_ref, e_ref, y_out, z_out):
-    del e_in
-    add_sources(e_ref, 2, cell_ref, mine_ref[...] * line_ref[0:1, :], cell_ref.shape[0])
-    electric_edges(e_ref, y_out, z_out)
+    values = fetch(cur_tab, owner >> 7, owner & (LANES - 1))[0:1] * line_ref[0:1, :]
+    add_sources(e_ref, (2,), cell_ref, values, same_ref, mark_ref, work)
+    electric_edges(
+        e_ref.shape[1],
+        lambda c, i: e_ref[2 * c, i, 0:1, :],
+        lambda c, i: e_ref[c, i, :, 0:LANES],
+        y_out,
+        z_out,
+    )
 
 
 def body(
@@ -467,7 +579,6 @@
     slots = port_cell.shape[0]
     devices = lax.axis_size(ALL)
     rows, ports = residues.shape[2:]
-    where = jnp.stack([lax.axis_index(name) for name in ALL]).astype(I32)
     y_edge, z_edge = ((2 * nx, nz), F32), ((ny, LANES), F32)
     table = pltpu.VMEM((8, LANES), F32)
     cells = port_cell.reshape(1, slots)
@@ -479,77 +590,112 @@
     def edges_on(y, z):
         return shifted(y, ("gx", "gy"), 1), shifted(z, "gz", 1)
 
-    def magnetic(electric, old, y, z):
-        return call(
-            h_kernel, ((field, F32), y_edge, z_edge), (VMEM,) * 7, (table,)
-        )(electric, old, material, decay_table, curl_table, y, z)
-
+    pair = ((2,) + material.shape, F32)
     send, y, z = call(
-        sample_kernel, (((devices, LANES), F32), y_edge, z_edge), (VMEM, SMEM, VMEM)
-    )(e_field, port_cell, owners)
+        sample_kernel,
+        (((devices, LANES), F32), y_edge, z_edge),
+        (HBM, HBM, HBM),
+        (
+            pltpu.SMEM((slots,), I32),
+            pltpu.VMEM((1, slots), I32),
+            pltpu.VMEM((slots, 8, nz), F32),
+            pltpu.VMEM((2, nx, 8, nz), F32),
+            pltpu.VMEM((2, nx, ny, LANES), F32),
+            pltpu.SemaphoreType.DMA((6,)),
+        ),
+    )(in_hbm(e_field), in_hbm(port_cell), in_hbm(owners))
+    recv = lax.all_to_all(send, ALL, 0, 0, tiled=True)
+    recv, y, z, fade, cells, curl_now = lax.optimization_barrier(
+        (recv, y, z, pole_decay, cells, curl_table)
+    )
     y, z = edges_back(y, z)
-    recv = lax.all_to_all(send, ALL, 0, 0, tiled=True)
+    magn, elec, e_held, h_held = call(
+        factor_kernel,
+        (pair, pair, (field, F32), (field, F32)),
+        (HBM,) * 3 + (VMEM,) * 2 + (SMEM,),
+        (
+            table,
+            pltpu.VMEM(material.shape, I32),
+            pltpu.SemaphoreType.DMA((4,)),
+            pltpu.SemaphoreType.DMA((2,)),
+        ),
+    )(in_hbm(material), in_hbm(e_field), in_hbm(h_field), decay_table, curl_table, curl_now)
+    y, z, magn = lax.optimization_barrier((y, z, magn))
+    h_one, y, z = call(h_kernel, ((field, F32), y_edge, z_edge), (VMEM,) * 5)(
+        e_held, h_held, magn, y, z
+    )
+    y, z = edges_on(y, z)
     sums, damped, base = call(
         residue_kernel,
         (((rows, ports), F32), ((rows, ports), F32), ((8, rows), F32)),
         (VMEM, SMEM, VMEM),
         (pltpu.VMEM((8, ports), F32), pltpu.VMEM((2, rows, LANES), F32)),
-    )(residues, pole_decay, pole_states)
-    (line,) = call(slot_kernel, (((8, LANES), F32),), (VMEM, VMEM, SMEM, VMEM), (table,))(
-        material, curl_table, port_cell, cells
-    )
-    h_one, y, z = magnetic(e_field, h_field, y, z)
-    y, z = edges_on(y, z)
+    )(residues, fade, pole_states)
+    line, same, mark = call(
+        slot_kernel,
+        (((8, LANES), F32), ((slots, slots), F32), ((slots, nz), F32)),
+        (VMEM, VMEM, SMEM, VMEM),
+        (table,),
+    )(material, curl_table, port_cell, cells)
     own, at, volts, current = call(
         first_kernel,
         (((64, LANES), I32), ((2, 8, LANES), I32), ((8, LANES), F32), ((1, rows), F32)),
-        (VMEM, VMEM, VMEM, VMEM, SMEM),
+        (VMEM, VMEM, VMEM, VMEM),
         (pltpu.VMEM((64, LANES), F32),),
-    )(recv, sums, base, direct, where)
+    )(recv, sums, base, direct)
     e_one, got = call(
-        e_kernel, ((field, F32), ((1, LANES), F32)), (VMEM,) * 7 + (SMEM,), (table,)
-    )(e_field, h_one, material, decay_table, curl_table, y, z, port_cell)
+        e_kernel, ((field, F32), ((1, LANES), F32)), (VMEM,) * 5 + (SMEM,)
+    )(e_held, h_one, elec, y, z, port_cell)
     (send,) = call(pack_kernel, (((4 * devices, LANES), F32),), (VMEM,) * 3)(got, line, current)
     recv = lax.all_to_all(send, ALL, 0, 0, tiled=True)
-    states, send, mine = call(
+    work = pltpu.VMEM((slots, nz), F32)
+    e_one, y, z, currents = call(
+        source_kernel,
+        ((field, F32), y_edge, z_edge, ((64, LANES), F32)),
+        (VMEM, VMEM, VMEM, VMEM, SMEM, VMEM, VMEM),
+        (work,),
+        aliases={0: 0},
+    )(e_one, recv, owners, line, port_cell, same, mark)
+    y, z = edges_back(y, z)
+    states, send = call(
         second_kernel,
-        ((pole_states.shape, F32), ((devices, LANES), F32), ((1, LANES), F32)),
-        (VMEM,) * 8 + (SMEM, VMEM, VMEM, SMEM),
+        ((pole_states.shape, F32), ((devices, LANES), F32)),
+        (VMEM,) * 9 + (SMEM, VMEM),
         (
             pltpu.VMEM((64, LANES), F32),
             pltpu.VMEM((64, LANES), F32),
             pltpu.VMEM((64, LANES), F32),
-            pltpu.VMEM((72, LANES), F32),
+            pltpu.VMEM((64, LANES), F32),
+            pltpu.VMEM((8, LANES), F32),
             pltpu.VMEM((8, LANES), F32),
         ),
-    )(recv, own, at, volts, sums, damped, base, direct, pole_decay, pole_states, owners, where)
-    e_one, y, z = call(
-        source_kernel, ((field, F32), y_edge, z_edge), (VMEM, VMEM, VMEM, SMEM), aliases={0: 0}
-    )(e_one, mine, line, port_cell)
-    y, z = edges_back(y, z)
+    )(recv, currents, own, at, volts, sums, damped, base, direct, pole_decay, pole_states)
+    send, y, z = lax.optimization_barrier((send, y, z))
+    h_two, y, z = call(h_kernel, ((field, F32), y_edge, z_edge), (VMEM,) * 5)(
+        e_one, h_one, magn, y, z
+    )
+    y, z = edges_on(y, z)
     recv = lax.all_to_all(send, ALL, 0, 0, tiled=True)
-    h_two, y, z = magnetic(e_one, h_one, y, z)
-    y, z = edges_on(y, z)
+    recv, y, z = lax.optimization_barrier((recv, y, z))
     e_out, h_out, ez = call(
         e_last_kernel,
         ((field, F32), (field, F32), (field[1:], F32)),
-        (VMEM,) * 7,
+        (VMEM,) * 5,
         (
-            table,
             pltpu.VMEM((2,) + field[1:], F32),
             pltpu.SemaphoreType.DMA((2,)),
             pltpu.SemaphoreType.DMA,
         ),
-        specs_out=(ANY, ANY, VMEM),
-    )(e_one, h_two, material, decay_table, curl_table, y, z)
-    (e_out,) = call(
+        specs_out=(HBM, HBM, VMEM),
+    )(e_one, h_two, elec, y, z)
+    e_out, _ = call(
         finish_kernel,
-        ((field, F32),),
-        (ANY, VMEM, VMEM, VMEM, SMEM),
-        (pltpu.VMEM((1,) + field[1:], F32), pltpu.SemaphoreType.DMA),
-        aliases={0: 0},
-        specs_out=(ANY,),
-    )(e_out, ez, recv, line[0:1], port_cell)
+        ((field, F32), (field[1:], F32)),
+        (HBM, VMEM, VMEM, VMEM, SMEM, VMEM, VMEM),
+        (work, pltpu.SemaphoreType.DMA),
+        aliases={0: 0, 1: 1},
+        specs_out=(HBM, VMEM),
+    )(e_out, ez, recv, line, port_cell, same, mark)
     return e_out, h_out, states
 
 

time: 135 us -> 127 us (0.941)
  blocking collectives: 17.8 us -> 32.6 us
  Pallas kernels: 44.6 us -> 32.4 us
  local copies, waits for them, and re-layouts: 23 us -> 15.7 us
  starting transfers between devices: 42.1 us -> 35.6 us
  waiting for transfers between devices: 6.04 us -> 9.29 us
    all_to_all x1 -> x2, blocking collectives: 17.8 us -> 32.6 us  [body(): recv = lax.all_to_all(send, ALL, 0, 0, tiled=True)]
    pallas_call x8 -> x9, Pallas kernels: 35.1 us -> 26 us  [the longest x2 7.37 us: body(): call(h_kernel, ((field, F32), y_edge, z_edge), (VMEM,) * 5)]
    unnamed x46 -> x36, local copies, waits for them, and re-layouts: 23 us -> 15.7 us
    all_to_all x2 -> x1, starting transfers between devices: 17.4 us -> 10.4 us  [body(): recv = lax.all_to_all(send, ALL, 0, 0, tiled=True)]
    ppermute x8, waiting for transfers between devices: 6.03 us -> 9.29 us  [shifted(): lax.ppermute(value, axis, [(source, source + steps) for source in range(i...]
    pallas_call x1, Pallas kernels: 5.87 us -> 3.12 us  [body(): call(e_last_kernel, ((field, F32), (field, F32), (field[1:], F32)), (VMEM...]
  transfers between devices with their start and end apart: 10 -> 9, of which waited for: 1 -> 2; matrix products, arithmetic and copies ran while one was open for 0% -> 0% of each run, Pallas kernels for 18% -> 12%
where the time goes in v2:
time: 127 us
  starting transfers between devices  35.6 us (28%)
  blocking collectives  32.6 us (26%)
  Pallas kernels  32.4 us (26%)
  local copies, waits for them, and re-layouts  15.7 us (12%)
  waiting for transfers between devices  9.29 us (7%)
    all_to_all x2, blocking collectives, body(): recv = lax.all_to_all(send, ALL, 0, 0, tiled=True)  32.6 us
    ppermute x8, starting transfers between devices, shifted(): lax.ppermute(value, axis, [(source, source + steps) for source in range(i...  25.2 us
    unnamed x36, local copies, waits for them, and re-layouts  15.7 us
    all_to_all x1, starting transfers between devices, body(): recv = lax.all_to_all(send, ALL, 0, 0, tiled=True)  10.4 us
    ppermute x8, waiting for transfers between devices, shifted(): lax.ppermute(value, axis, [(source, source + steps) for source in range(i...  9.29 us
    pallas_call x2, Pallas kernels, body(): call(h_kernel, ((field, F32), y_edge, z_edge), (VMEM,) * 5)  7.37 us
    pallas_call x1, Pallas kernels, body(): call(factor_kernel, (pair, pair, (field, F32), (field, F32)), (HBM,) * 3...  5.63 us
    pallas_call x1, Pallas kernels, body(): call(e_last_kernel, ((field, F32), (field, F32), (field[1:], F32)), (VMEM...  3.12 us
  transfers between devices with their start and end apart: 9, of which 2 were waited for; matrix products, arithmetic and copies ran while one was open for 0% of the time, Pallas kernels for 12%

profile of v2, /device:TPU:64, one launch (start us, length us, event | category | flops | bytes accessed | tf_op | source)
XLA Modules:
  0.0 126.5 jit_solution(16558053787699207123)
XLA Ops:
  0.7 3.0 %shard_map.130 = (f32[128,128]{1,0:T(8,128)S(1)}, f32[48,256]{1,0:T(8,128)S(1)}, f32[64,128]{1,0:T(8,128)S(1)}) custom-call(f32[3,24,64,256]{3,2,1,0:T(8,128)} %e_in.1, s32[64]{0:T(128)} %cell_ref.7, s32[1,64]{1,0:T(1,128)} %bitcast.19), custom_call_target="tpu_custom_call" | custom-call | tf_op jit(solution)/shard_map/pallas_call | solution.py:594
  3.7 17.5 %all_to_all.35 = f32[128,1,128]{2,1,0:T(1,128)S(1)} all-to-all(f32[128,1,128]{2,1,0:T(1,128)S(1)} %bitcast.17), channel_id=1, replica_groups=mesh['gx'=4,'gy'=4,'gz'=8] {'gx','gy','gz'}, dimensions={0} | all-to-all | bytes 131072 | tf_op jit(solution)/shard_map/all_to_all | solution.py:607
  22.4 4.6 %collective-permute-start.1 = (f32[64,128]{1,0:T(8,128)S(1)}, f32[64,128]{1,0:T(8,128)S(1)}, u32[]{:S(2)}, u32[]{:S(2)}) collective-permute-start(f32[64,128]{1,0:T(8,128)S(1)} %get-tuple-element.60), channel_id=1, source_target_pairs={{1,0},{2,1},{3,2},{4,3},{5,4},{6,5},{7,6},{9,8},{10,9},{11,10},{12... | collective-permute-start | bytes 98312 | tf_op jit(solution)/shard_map/ppermute | solution.py:38
  27.1 5.6 %shard_map.131 = (f32[2,24,64,256]{3,2,1,0:T(8,128)S(1)}, f32[2,24,64,256]{3,2,1,0:T(8,128)S(1)}, f32[3,24,64,256]{3,2,1,0:T(8,128)S(1)}, f32[3,24,64,256]{3,2,1,0:T(8,128)S(1)}) custom-call(s32[24,64,256]{2,1,0:T(8,128)} %mat_ref.1, f32[3,24,64,256]{3,2,1,0:T(8,128)} %e_in.1, f32[3,24,64,256]{3,2,1,0:T(8,128)} %h_in.1, f32[2,16]{1,0:T(2,128)S(1)} %copy-done.17, ...), custom_call_target="tpu_custom_call" | custom-call | tf_op jit(solution)/shard_map/pallas_call | solution.py:612
  32.8 3.8 %shard_map.132 = (f32[3,24,64,256]{3,2,1,0:T(8,128)S(1)}, f32[48,256]{1,0:T(8,128)S(1)}, f32[64,128]{1,0:T(8,128)S(1)}) custom-call(f32[3,24,64,256]{3,2,1,0:T(8,128)S(1)} %get-tuple-element.57.e_ref, f32[3,24,64,256]{3,2,1,0:T(8,128)S(1)} %get-tuple-element.58.h_ref, f32[2,24,64,256]{3,2,1,0:T(8,128)S(1)} %get-tuple-element.62.magn_ref, ...), custom_call_target="tpu_custom_call" | custom-call | tf_op jit(solution)/shard_map/pallas_call | solution.py:624
  36.6 4.7 %collective-permute-start.2 = (f32[48,256]{1,0:T(8,128)S(1)}, f32[48,256]{1,0:T(8,128)S(1)}, u32[]{:S(2)}, u32[]{:S(2)}) collective-permute-start(f32[48,256]{1,0:T(8,128)S(1)} %get-tuple-element.67), channel_id=1, source_target_pairs={{0,8},{8,16},{16,24},{24,32},{32,40},{40,48},{48,56},{56,64},{64,7... | collective-permute-start | bytes 147464 | tf_op jit(solution)/shard_map/ppermute | solution.py:38
  44.3 2.1 %shard_map.135 = (f32[256,1024]{1,0:T(8,128)S(1)}, f32[256,1024]{1,0:T(8,128)S(1)}, f32[8,256]{1,0:T(8,128)S(1)}) custom-call(f32[1,4,256,1024]{3,2,1,0:T(8,128)S(1)} %copy-done.10, f32[1,4]{1,0:T(1,128)S(1)} %copy-done.16, f32[1,4,1024]{2,1,0:T(4,128)S(1)} %copy-done.11), custom_call_target="tpu_custom_call" | custom-call | tf_op jit(solution)/shard_map/pallas_call | solution.py:628
  47.5 3.2 %collective-permute-done.3.zl_ref = f32[64,128]{1,0:T(8,128)S(1)} collective-permute-done((f32[64,128]{1,0:T(8,128)S(1)}, f32[64,128]{1,0:T(8,128)S(1)}, u32[]{:S(2)}, u32[]{:S(2)}) %collective-permute-start.3) | collective-permute-done | bytes 32800 | tf_op jit(solution)/shard_map/ppermute | solution.py:38
  50.7 3.0 %shard_map.133 = (f32[3,24,64,256]{3,2,1,0:T(8,128)S(1)}, f32[1,128]{1,0:T(1,128)S(1)}) custom-call(f32[3,24,64,256]{3,2,1,0:T(8,128)S(1)} %get-tuple-element.57.e_ref, f32[3,24,64,256]{3,2,1,0:T(8,128)S(1)} %get-tuple-element.65.h_ref, f32[2,24,64,256]{3,2,1,0:T(8,128)S(1)} %get-tuple-element.66.elec_ref, f32[48,256]{1,0:T(8,128)S(1)} %collective-permute-done.2.yl_ref, ...), custom_call_target="tpu_custom_call" | custom-call | tf_op jit(solution)/shard_map/pallas_call | solution.py:646
  53.9 15.2 %all_to_all.36 = f32[128,4,128]{2,1,0:T(4,128)S(1)} all-to-all(f32[128,4,128]{2,1,0:T(4,128)S(1)} %bitcast.14), channel_id=1, replica_groups=mesh['gx'=4,'gy'=4,'gz'=8] {'gx','gy','gz'}, dimensions={0} | all-to-all | bytes 524288 | tf_op jit(solution)/shard_map/all_to_all | solution.py:650
  70.9 2.2 %copy-done = f32[3,24,64,256]{3,2,1,0:T(8,128)} copy-done((f32[3,24,64,256]{3,2,1,0:T(8,128)}, f32[3,24,64,256]{3,2,1,0:T(8,128)S(1)}, u32[]{:S(2)}) %copy-start) | copy-done | bytes 4718616
  74.4 4.6 %collective-permute-start.5 = (f32[64,128]{1,0:T(8,128)S(1)}, f32[64,128]{1,0:T(8,128)S(1)}, u32[]{:S(2)}, u32[]{:S(2)}) collective-permute-start(f32[64,128]{1,0:T(8,128)S(1)} %get-tuple-element.88), channel_id=1, source_target_pairs={{1,0},{2,1},{3,2},{4,3},{5,4},{6,5},{7,6},{9,8},{10,9},{11,10},{12... | collective-permute-start | bytes 98312 | tf_op jit(solution)/shard_map/ppermute | solution.py:38
  80.9 10.4 %all-to-all-start.2 = ((f32[128,1,128]{2,1,0:T(1,128)}), f32[128,1,128]{2,1,0:T(1,128)S(1)}, u32[]{:S(2)}, u32[]{:S(2)}) async-start(f32[128,1,128]{2,1,0:T(1,128)} %bitcast.8), calls=%async_computation.2 | async-start | bytes 131072 | tf_op jit(solution)/shard_map/all_to_all | solution.py:678
  91.3 2.3 %copy-done.1 = f32[3,24,64,256]{3,2,1,0:T(8,128)S(1)} copy-done((f32[3,24,64,256]{3,2,1,0:T(8,128)S(1)}, f32[3,24,64,256]{3,2,1,0:T(8,128)}, u32[]{:S(2)}) %copy-start.1) | copy-done | bytes 4718616
  93.7 2.3 %copy-done.4 = f32[3,24,64,256]{3,2,1,0:T(8,128)S(1)} copy-done((f32[3,24,64,256]{3,2,1,0:T(8,128)S(1)}, f32[3,24,64,256]{3,2,1,0:T(8,128)}, u32[]{:S(2)}) %copy-start.4) | copy-done | bytes 4718616
  97.9 3.6 %shard_map.140 = (f32[3,24,64,256]{3,2,1,0:T(8,128)S(1)}, f32[48,256]{1,0:T(8,128)S(1)}, f32[64,128]{1,0:T(8,128)S(1)}) custom-call(f32[3,24,64,256]{3,2,1,0:T(8,128)S(1)} %copy-done.1, f32[3,24,64,256]{3,2,1,0:T(8,128)S(1)} %copy-done.4, f32[2,24,64,256]{3,2,1,0:T(8,128)S(1)} %copy-done.6, f32[48,256]{1,0:T(8,128)S(1)} %collective-permute-done.4.yh_ref, ...), custom_call_target="tpu_custom_call" | custom-call | tf_op jit(solution)/shard_map/pallas_call | solution.py:674
  101.5 2.2 %copy-done.8 = f32[3,24,64,256]{3,2,1,0:T(8,128)} copy-done((f32[3,24,64,256]{3,2,1,0:T(8,128)}, f32[3,24,64,256]{3,2,1,0:T(8,128)S(1)}, u32[]{:S(2)}) %copy-start.8) | copy-done | bytes 4718616
  103.7 3.4 %collective-permute-start.6 = (f32[48,256]{1,0:T(8,128)S(1)}, f32[48,256]{1,0:T(8,128)S(1)}, u32[]{:S(2)}, u32[]{:S(2)}) collective-permute-start(f32[48,256]{1,0:T(8,128)S(1)} %get-tuple-element.93), channel_id=1, source_target_pairs={{0,8},{8,16},{16,24},{24,32},{32,40},{40,48},{48,56},{56,64},{64,7... | collective-permute-start | bytes 147464 | tf_op jit(solution)/shard_map/ppermute | solution.py:38
  107.1 3.4 %collective-permute-start.7 = (f32[64,128]{1,0:T(8,128)S(1)}, f32[64,128]{1,0:T(8,128)S(1)}, u32[]{:S(2)}, u32[]{:S(2)}) collective-permute-start(f32[64,128]{1,0:T(8,128)S(1)} %get-tuple-element.94), channel_id=1, source_target_pairs={{0,1},{1,2},{2,3},{3,4},{4,5},{5,6},{6,7},{8,9},{9,10},{10,11},{11... | collective-permute-start | bytes 98312 | tf_op jit(solution)/shard_map/ppermute | solution.py:38
  110.5 6.0 %collective-permute-done.7.zl_ref = f32[64,128]{1,0:T(8,128)S(1)} collective-permute-done((f32[64,128]{1,0:T(8,128)S(1)}, f32[64,128]{1,0:T(8,128)S(1)}, u32[]{:S(2)}, u32[]{:S(2)}) %collective-permute-start.7) | collective-permute-done | bytes 32800 | tf_op jit(solution)/shard_map/ppermute | solution.py:38
  116.5 2.3 %copy-done.2 = f32[3,24,64,256]{3,2,1,0:T(8,128)S(1)} copy-done((f32[3,24,64,256]{3,2,1,0:T(8,128)S(1)}, f32[3,24,64,256]{3,2,1,0:T(8,128)}, u32[]{:S(2)}) %copy-start.2) | copy-done | bytes 4718616
  118.9 2.3 %copy-done.9 = f32[3,24,64,256]{3,2,1,0:T(8,128)S(1)} copy-done((f32[3,24,64,256]{3,2,1,0:T(8,128)S(1)}, f32[3,24,64,256]{3,2,1,0:T(8,128)}, u32[]{:S(2)}) %copy-start.9) | copy-done | bytes 4718616
  121.2 3.1 %shard_map.141 = (f32[3,24,64,256]{3,2,1,0:T(8,128)}, f32[3,24,64,256]{3,2,1,0:T(8,128)}, f32[24,64,256]{2,1,0:T(8,128)S(1)}) custom-call(f32[3,24,64,256]{3,2,1,0:T(8,128)S(1)} %copy-done.2, f32[3,24,64,256]{3,2,1,0:T(8,128)S(1)} %copy-done.9, f32[2,24,64,256]{3,2,1,0:T(8,128)S(1)} %get-tuple-element.66.elec_ref, ...), custom_call_target="tpu_custom_call" | custom-call | tf_op jit(solution)/shard_map/pallas_call | solution.py:680
  124.3 2.2 %shard_map.142 = (f32[3,24,64,256]{3,2,1,0:T(8,128)}, f32[24,64,256]{2,1,0:T(8,128)S(1)}) custom-call(f32[3,24,64,256]{3,2,1,0:T(8,128)} %get-tuple-element.97.e_in, f32[24,64,256]{2,1,0:T(8,128)S(1)} %get-tuple-element.98.ez_in, f32[128,128]{1,0:T(8,128)S(1)} %bitcast.15, ...), custom_call_target="tpu_custom_call", output_to_operand_aliasing={{0}: (0, {}), {1}: (1, {})} | custom-call | tf_op jit(solution)/shard_map/pallas_call | solution.py:691
  (45 shorter events, 12.4 us)
Async XLA Ops:
  0.6 26.4 %copy-start.13 = (f32[2,16]{1,0:T(2,128)S(1)}, f32[2,16]{1,0:T(2,128)}, u32[]{:S(2)}) copy-start(f32[2,16]{1,0:T(2,128)} %curl_ref.3) | copy-start | bytes 388
  0.6 26.4 %copy-start.17 = (f32[2,16]{1,0:T(2,128)S(1)}, f32[2,16]{1,0:T(2,128)}, u32[]{:S(2)}) copy-start(f32[2,16]{1,0:T(2,128)} %decay_ref.2) | copy-start | bytes 388
  21.1 11.6 %collective-permute-start = (f32[48,256]{1,0:T(8,128)S(1)}, f32[48,256]{1,0:T(8,128)S(1)}, u32[]{:S(2)}, u32[]{:S(2)}) collective-permute-start(f32[48,256]{1,0:T(8,128)S(1)} %get-tuple-element.59), channel_id=1, source_target_pairs={{8,0},{16,8},{24,16},{32,24},{40,32},{48,40},{56,48},{64,56},{72,6... | collective-permute-start | bytes 147464 | tf_op jit(solution)/shard_map/ppermute | solution.py:38
  22.4 10.3 %collective-permute-start.1 = (f32[64,128]{1,0:T(8,128)S(1)}, f32[64,128]{1,0:T(8,128)S(1)}, u32[]{:S(2)}, u32[]{:S(2)}) collective-permute-start(f32[64,128]{1,0:T(8,128)S(1)} %get-tuple-element.60), channel_id=1, source_target_pairs={{1,0},{2,1},{3,2},{4,3},{5,4},{6,5},{7,6},{9,8},{10,9},{11,10},{12... | collective-permute-start | bytes 98312 | tf_op jit(solution)/shard_map/ppermute | solution.py:38
  32.7 3.9 %copy-start.5 = (f32[2,24,64,256]{3,2,1,0:T(8,128)}, f32[2,24,64,256]{3,2,1,0:T(8,128)S(1)}, u32[]{:S(2)}) copy-start(f32[2,24,64,256]{3,2,1,0:T(8,128)S(1)} %get-tuple-element.62.magn_ref) | copy-start | bytes 9437188
  32.7 10.5 %copy-start.7 = (s32[24,64,256]{2,1,0:T(8,128)S(1)}, s32[24,64,256]{2,1,0:T(8,128)}, u32[]{:S(2)}) copy-start(s32[24,64,256]{2,1,0:T(8,128)} %mat_ref.1) | copy-start | bytes 4718596
  32.8 10.5 %copy-start.12 = (s32[64]{0:T(128)S(1)}, s32[64]{0:T(128)}, u32[]{:S(2)}) copy-start(s32[64]{0:T(128)} %cell_ref.7) | copy-start | bytes 772
  32.8 11.5 %copy-start.10 = (f32[1,4,256,1024]{3,2,1,0:T(8,128)S(1)}, f32[1,4,256,1024]{3,2,1,0:T(8,128)}, u32[]{:S(2)}) copy-start(f32[1,4,256,1024]{3,2,1,0:T(8,128)} %res_ref.1) | copy-start | bytes 12582916
  32.8 11.5 %copy-start.11 = (f32[1,4,1024]{2,1,0:T(4,128)S(1)}, f32[1,4,1024]{2,1,0:T(4,128)}, u32[]{:S(2)}) copy-start(f32[1,4,1024]{2,1,0:T(4,128)} %state_ref.3) | copy-start | bytes 49156
  32.8 11.5 %copy-start.16 = (f32[1,4]{1,0:T(1,128)S(1)}, f32[1,4]{1,0:T(1,128)}, u32[]{:S(2)}) copy-start(f32[1,4]{1,0:T(1,128)} %decay_ref.4) | copy-start | bytes 52
  36.6 17.2 %copy-start.3 = (f32[3,24,64,256]{3,2,1,0:T(8,128)}, f32[3,24,64,256]{3,2,1,0:T(8,128)S(1)}, u32[]{:S(2)}) copy-start(f32[3,24,64,256]{3,2,1,0:T(8,128)S(1)} %get-tuple-element.65.h_ref) | copy-start | bytes 14155780
  36.6 9.8 %copy-start.14 = (f32[1,256]{1,0:T(1,128)S(1)}, f32[1,256]{1,0:T(1,128)}, u32[]{:S(2)}) copy-start(f32[1,256]{1,0:T(1,128)} %direct_ref.3) | copy-start | bytes 3076
  36.6 14.1 %collective-permute-start.2 = (f32[48,256]{1,0:T(8,128)S(1)}, f32[48,256]{1,0:T(8,128)S(1)}, u32[]{:S(2)}, u32[]{:S(2)}) collective-permute-start(f32[48,256]{1,0:T(8,128)S(1)} %get-tuple-element.67), channel_id=1, source_target_pairs={{0,8},{8,16},{16,24},{24,32},{32,40},{40,48},{48,56},{56,64},{64,7... | collective-permute-start | bytes 147464 | tf_op jit(solution)/shard_map/ppermute | solution.py:38
  41.3 9.4 %collective-permute-start.3 = (f32[64,128]{1,0:T(8,128)S(1)}, f32[64,128]{1,0:T(8,128)S(1)}, u32[]{:S(2)}, u32[]{:S(2)}) collective-permute-start(f32[64,128]{1,0:T(8,128)S(1)} %get-tuple-element.68), channel_id=1, source_target_pairs={{0,1},{1,2},{2,3},{3,4},{4,5},{5,6},{6,7},{8,9},{9,10},{10,11},{11... | collective-permute-start | bytes 98312 | tf_op jit(solution)/shard_map/ppermute | solution.py:38
  50.7 18.3 %copy-start.15 = (s32[64]{0:T(128)S(1)}, s32[64]{0:T(128)}, u32[]{:S(2)}) copy-start(s32[64]{0:T(128)} %param.21) | copy-start | bytes 772
  73.1 7.8 %collective-permute-start.4 = (f32[48,256]{1,0:T(8,128)S(1)}, f32[48,256]{1,0:T(8,128)S(1)}, u32[]{:S(2)}, u32[]{:S(2)}) collective-permute-start(f32[48,256]{1,0:T(8,128)S(1)} %get-tuple-element.87), channel_id=1, source_target_pairs={{8,0},{16,8},{24,16},{32,24},{40,32},{48,40},{56,48},{64,56},{72,6... | collective-permute-start | bytes 147464 | tf_op jit(solution)/shard_map/ppermute | solution.py:38
  74.4 6.5 %collective-permute-start.5 = (f32[64,128]{1,0:T(8,128)S(1)}, f32[64,128]{1,0:T(8,128)S(1)}, u32[]{:S(2)}, u32[]{:S(2)}) collective-permute-start(f32[64,128]{1,0:T(8,128)S(1)} %get-tuple-element.88), channel_id=1, source_target_pairs={{1,0},{2,1},{3,2},{4,3},{5,4},{6,5},{7,6},{9,8},{10,9},{11,10},{12... | collective-permute-start | bytes 98312 | tf_op jit(solution)/shard_map/ppermute | solution.py:38
  80.9 35.6 %all-to-all-start.2 = ((f32[128,1,128]{2,1,0:T(1,128)}), f32[128,1,128]{2,1,0:T(1,128)S(1)}, u32[]{:S(2)}, u32[]{:S(2)}) async-start(f32[128,1,128]{2,1,0:T(1,128)} %bitcast.8), calls=%async_computation.2 | async-start | bytes 131072 | tf_op jit(solution)/shard_map/all_to_all | solution.py:678
  91.3 2.3 %copy-start.1 = (f32[3,24,64,256]{3,2,1,0:T(8,128)S(1)}, f32[3,24,64,256]{3,2,1,0:T(8,128)}, u32[]{:S(2)}) copy-start(f32[3,24,64,256]{3,2,1,0:T(8,128)} %copy-done) | copy-start | bytes 14155780
  93.7 2.3 %copy-start.4 = (f32[3,24,64,256]{3,2,1,0:T(8,128)S(1)}, f32[3,24,64,256]{3,2,1,0:T(8,128)}, u32[]{:S(2)}) copy-start(f32[3,24,64,256]{3,2,1,0:T(8,128)} %copy-done.3) | copy-start | bytes 14155780
  103.7 12.9 %collective-permute-start.6 = (f32[48,256]{1,0:T(8,128)S(1)}, f32[48,256]{1,0:T(8,128)S(1)}, u32[]{:S(2)}, u32[]{:S(2)}) collective-permute-start(f32[48,256]{1,0:T(8,128)S(1)} %get-tuple-element.93), channel_id=1, source_target_pairs={{0,8},{8,16},{16,24},{24,32},{32,40},{40,48},{48,56},{56,64},{64,7... | collective-permute-start | bytes 147464 | tf_op jit(solution)/shard_map/ppermute | solution.py:38
  107.1 9.4 %collective-permute-start.7 = (f32[64,128]{1,0:T(8,128)S(1)}, f32[64,128]{1,0:T(8,128)S(1)}, u32[]{:S(2)}, u32[]{:S(2)}) collective-permute-start(f32[64,128]{1,0:T(8,128)S(1)} %get-tuple-element.94), channel_id=1, source_target_pairs={{0,1},{1,2},{2,3},{3,4},{4,5},{5,6},{6,7},{8,9},{9,10},{10,11},{11... | collective-permute-start | bytes 98312 | tf_op jit(solution)/shard_map/ppermute | solution.py:38
  116.5 2.3 %copy-start.2 = (f32[3,24,64,256]{3,2,1,0:T(8,128)S(1)}, f32[3,24,64,256]{3,2,1,0:T(8,128)}, u32[]{:S(2)}) copy-start(f32[3,24,64,256]{3,2,1,0:T(8,128)} %copy-done) | copy-start | bytes 14155780
  118.9 2.3 %copy-start.9 = (f32[3,24,64,256]{3,2,1,0:T(8,128)S(1)}, f32[3,24,64,256]{3,2,1,0:T(8,128)}, u32[]{:S(2)}) copy-start(f32[3,24,64,256]{3,2,1,0:T(8,128)} %copy-done.8) | copy-start | bytes 14155780
  (3 other events, 6.3 us)
